TPU v7x, 256 devices: a whole 4x4x8 slice. The times are simulated.
256 devices in a mesh: freq: 32 (over z, y), row: 2 (over x_lo), col: 4 (over x_hi, core).
Axes of the slice: x: 4 (x_hi: 2, x_lo: 2; x = x_hi * 2 + x_lo), y: 4, z: 8, core: 2. Of those that a mesh axis runs over, the one named last changes fastest.
Arguments:
- samples: int32 [2, 2048, 68608], P(None, ('row', 'col', 'freq')), may hold values from -7 to 7
- input_gains: float32 [2048], P(('row', 'col', 'freq')), may hold values from 0.3 to 3
- filter_taps: float32 [4, 1024], replicated, may hold values from 0.25 to 1
Outputs:
- vis_real: bfloat16 [128, 2048, 2048], P('freq', 'row', 'col')
- vis_imag: bfloat16 [128, 2048, 2048], P('freq', 'row', 'col')
All inputs are finite; a program needn't handle non-finite values.
Results may differ from a plain program's by a relative error of at most 0.0065.
Values may be sent and summed in bfloat16 or wider, within the bound.
A program may use at most 64 MiB of HBM per device.

v0:
```python
import math

import jax
import jax.numpy as jnp
from jax import lax
from jax.sharding import PartitionSpec as P

NFFT = 1024
TAPS = 4
SPEC = 64
CH_DEV = 4


def dft_table(channels):
    position = jnp.arange(NFFT, dtype=jnp.int32)
    channel = jnp.arange(channels, dtype=jnp.int32)
    phases = (position[:, None] * channel[None, :] % NFFT).astype(jnp.float32) * (
        2.0 * math.pi / NFFT
    )
    scaling = 0.5 / math.sqrt(NFFT)
    cosine = jnp.cos(phases) * scaling
    sine = jnp.sin(phases) * scaling
    real_rows = jnp.stack([cosine, -sine], axis=1)
    imag_rows = jnp.stack([sine, cosine], axis=1)
    return jnp.stack([real_rows, imag_rows], axis=0).astype(jnp.bfloat16)


def local(samples, input_gains, filter_taps):
    channels = CH_DEV * lax.axis_size("freq")
    inputs_here = samples.shape[1]
    voltage = samples.astype(jnp.float32) * 0.25 * input_gains[None, :, None]
    frames = voltage.reshape(2, inputs_here, SPEC + TAPS - 1, NFFT)
    filtered = frames[:, :, 0:SPEC, :] * filter_taps[0]
    for tap_index in range(1, TAPS):
        filtered = filtered + frames[:, :, tap_index : tap_index + SPEC, :] * filter_taps[tap_index]
    filtered = filtered.astype(jnp.bfloat16)
    spectra = jnp.einsum(
        "pimn,pnqk->kiqm", filtered, dft_table(channels), preferred_element_type=jnp.float32
    )
    spectra = spectra.reshape(channels, inputs_here, 2 * SPEC).astype(jnp.bfloat16)
    grouped = lax.all_to_all(spectra, "freq", split_axis=0, concat_axis=1, tiled=True)
    row_count = lax.axis_size("row")
    column_count = lax.axis_size("col")
    everything = lax.all_gather(grouped, ("row", "col"), axis=1, tiled=True)
    row_size = everything.shape[1] // row_count
    column_size = everything.shape[1] // column_count
    row_data = lax.dynamic_slice_in_dim(everything, lax.axis_index("row") * row_size, row_size, 1)
    column_data = lax.dynamic_slice_in_dim(
        everything, lax.axis_index("col") * column_size, column_size, 1
    )
    rotated = jnp.concatenate([-column_data[:, :, SPEC:], column_data[:, :, :SPEC]], axis=2)
    stacked = jnp.concatenate([column_data, rotated], axis=1)
    product = jnp.einsum("kim,kjm->kij", row_data, stacked, preferred_element_type=jnp.float32) * (
        1.0 / SPEC
    )
    width = column_data.shape[1]
    vis_real = product[:, :, :width].astype(jnp.bfloat16)
    vis_imag = product[:, :, width:].astype(jnp.bfloat16)
    return (vis_real, vis_imag)


def solution(mesh):
    placed = (P(None, ("row", "col", "freq"), None), P(("row", "col", "freq")), P())
    return jax.shard_map(
        local,
        mesh=mesh,
        in_specs=placed,
        out_specs=(P("freq", "row", "col"), P("freq", "row", "col")),
        check_vma=False,
    )
```

profile of v0, /device:TPU:1, one launch (start us, length us, event | category | flops | bytes accessed | tf_op | source)
XLA Modules:
  0.0 104.9 jit_solution(10403629546173163762)
XLA Ops:
  7.2 0.0 all-gather.2.cloned.1.call-start
  7.2 2.2 %negate_convert_fusion = (bf16[1024,1,128]{2,0,1:T(8,128)(2,1)S(1)}, bf16[1024,1,128]{2,0,1:T(8,128)(2,1)S(1)}) fusion(), kind=kLoop, calls=%fused_computation.33 | loop fusion | flops 2490368 | bytes 524288 | tf_op jit(solution)/shard_map/convert.9
  9.4 2.0 %fusion.30 = bf16[1024,1,128]{2,0,1:T(8,128)(2,1)S(1)} fusion(), kind=kLoop, calls=%fused_computation.39 | loop fusion | flops 2097152 | bytes 262144 | tf_op jit(solution)/shard_map/convert.5
  11.4 0.7 broadcast_multiply_fusion
  12.1 2.6 %convert_multiply_fusion = f32[2,8,68608]{2,1,0:T(8,128)S(1)} fusion(s32[2,8,68608]{2,1,0:T(8,128)} %param.3, f32[8]{0:T(128)S(1)} %broadcast_multiply_fusion), kind=kLoop, calls=%fused_computation.1 | loop fusion | flops 2195456 | bytes 8781856 | tf_op jit(solution)/shard_map/mul | solution.py:31
  14.7 0.0 copy-start
  14.7 3.5 %fusion.35 = (f32[2,8,64,1024]{3,1,2,0:T(8,128)S(1)}, f32[2,8,64,1024]{3,1,2,0:T(8,128)S(1)}, f32[2,8,64,1024]{3,1,2,0:T(8,128)S(1)}, f32[2,8,64,1024]{3,1,2,0:T(8,128)S(1)}) fusion(f32[2,8,67,1024]{3,1,2,0:T(8,128)S(1)} %bitcast.41), kind=kLoop, calls=%fused_computation.48 | loop fusion | bytes 33554432 | tf_op jit(solution)/shard_map/slice | solution.py:33
  18.3 0.0 copy-done
  18.3 0.1 maximum_bitcast_fusion.2
  18.4 9.9 %fusion.13 = bf16[128,8,2,64]{0,3,1,2:T(8,128)(2,1)S(1)} fusion(f32[1024]{0:T(1024)S(1)} %bitcast.47, f32[2,8,64,1024]{3,1,2,0:T(8,128)S(1)} %get-tuple-element.7, f32[1024]{0:T(1024)S(1)} %bitcast.48, f32[2,8,64,1024]{3,1,2,0:T(8,128)S(1)} %get-tuple-element.5, f32[1024]{0:T(1024)S(1)} %bitcast.46, f32[2,8,64,1024]{3,1,2,0:T(8,128)S(1)} %get-tuple-element.6, ...), kind=kOutput, calls=%fused_computation.14 | convolution fusion | flops 547487744 | bytes 18104320 | tf_op jit(solution)/shard_map/pimn,pnqk->kiqm/dot_general | solution.py:37
  28.3 0.2 copy.24
  28.5 23.0 %all_to_all.18 = bf16[128,8,128]{2,1,0:T(8,128)(2,1)S(1)} all-to-all(bf16[128,8,128]{2,1,0:T(8,128)(2,1)S(1)} %copy.24), channel_id=1, replica_groups=mesh['freq'=32,'row'=2,'col'=4] {'freq'}, dimensions={0} | all-to-all | bytes 524288 | tf_op jit(solution)/shard_map/all_to_all | solution.py:41
  51.6 0.7 copy.87
  52.3 0.0 all-gather.2.cloned.1.call-update
  52.3 35.7 %all-gather.2.cloned.1.call-done = bf16[4,2048,128]{2,1,0:T(8,128)(2,1)} async-done(((bf16[4,256,128]{2,1,0:T(8,128)(2,1)}), bf16[4,2048,128]{2,1,0:T(8,128)(2,1)}) %all-gather.2.cloned.1.call-update) | async-done | bytes 2097168 | tf_op jit(solution)/shard_map/all_gather | solution.py:44
  88.1 1.1 %constant_dynamic-slice_fusion.1 = bf16[4,512,128]{2,1,0:T(8,128)(2,1)S(1)} fusion(bf16[4,2048,128]{2,1,0:T(8,128)(2,1)} %all-gather.2.cloned.1.call-done, s32[]{:T(128)S(6)} %select_n.36), kind=kLoop, calls=%fused_computation.42 | loop fusion | bytes 1048580 | tf_op jit(solution)/shard_map/dynamic_slice | solution.py:48
  89.1 1.5 %dynamic-slice_negate_fusion = (bf16[4,512,64]{2,1,0:T(8,128)(2,1)S(1)}, bf16[4,512,64]{2,1,0:T(8,128)(2,1)S(1)}) fusion(bf16[4,2048,128]{2,1,0:T(8,128)(2,1)} %all-gather.2.cloned.1.call-done, s32[]{:T(128)S(6)} %select_n.36, s32[]{:T(128)S(6)} %add.48), kind=kLoop, calls=%fused_computation.30 | loop fusion | flops 393216 | bytes 1048584 | tf_op jit(solution)/shard_map/neg | solution.py:51
  90.6 3.6 %multiply_convert_fusion = bf16[4,1024,1024]{2,1,0:T(8,128)(2,1)S(1)} fusion(bf16[4,512,64]{2,1,0:T(8,128)(2,1)S(1)} %get-tuple-element.9, bf16[4,512,64]{2,1,0:T(8,128)(2,1)S(1)} %get-tuple-element.8, bf16[4,512,128]{2,1,0:T(8,128)(2,1)S(1)} %constant_dynamic-slice_fusion.1, bf16[4,2048,128]{2,1,0:T(8,128)(2,1)} %all-gather.2.cloned.1.call-done, s32[]{:T(128)S(6)} %select_n.35), kind=kOutput, calls=%fused_computation | convolution fusion | flops 1085276160 | bytes 10485764 | tf_op jit(solution)/shard_map/kim,kjm->kij/dot_general | solution.py:53
  94.2 3.9 %fusion.34 = (bf16[4,1024,512]{2,1,0:T(8,128)(2,1)}, bf16[4,1024,512]{2,1,0:T(8,128)(2,1)}) fusion(bf16[4,1024,1024]{2,1,0:T(8,128)(2,1)S(1)} %multiply_convert_fusion), kind=kLoop, calls=%fused_computation.47 | loop fusion | bytes 16777216 | tf_op jit(solution)/shard_map/slice | solution.py:58
  (2 shorter events, 0.1 us)
Async XLA Ops:
  7.2 80.9 %all-gather.2.cloned.1.call-start = ((), (), s32[]{:S(2)}) async-start(), calls=%async_computation.1 | async-start | bytes 2359296 | tf_op jit(solution)/shard_map/all_gather | solution.py:44
  14.7 3.6 %copy-start = (f32[4,1024]{1,0:T(4,128)S(1)}, f32[4,1024]{1,0:T(4,128)}, u32[]{:S(2)}) copy-start(f32[4,1024]{1,0:T(4,128)} %param.5) | copy-start | bytes 49156
Sparse Core Ops, SparseCore 0:
  52.5 35.5 all-gather.1
where the time goes:
time: 105 us
  waiting for transfers between devices  35.7 us (34%)
  blocking collectives  23 us (22%)
  between operations  14.1 us (13%)
  matrix products  13.5 us (13%)
  local copies, waits for them, and re-layouts  9.47 us (9%)
  other arithmetic  9.08 us (9%)
    all_gather x1, waiting for transfers between devices, local(): everything = lax.all_gather(grouped, ('row', 'col'), axis=1, tiled=True)  35.7 us
    all_to_all x1, blocking collectives, local(): lax.all_to_all(spectra, 'freq', split_axis=0, concat_axis=1, tiled=True)  23 us
    dot_general x1, matrix products, local(): jnp.einsum('pimn,pnqk->kiqm', filtered, dft_table(channels), preferred_el...  9.89 us
    another operation x2, other arithmetic  4.22 us
    slice x1, local copies, waits for them, and re-layouts, local(): vis_imag = product[:, :, width:].astype(jnp.bfloat16)  3.86 us
    dot_general x1, matrix products, local(): jnp.einsum('kim,kjm->kij', row_data, stacked, preferred_element_type=jnp....  3.59 us
    slice x2, local copies, waits for them, and re-layouts, local(): filtered = frames[:, :, 0:SPEC, :] * filter_taps[0]  3.55 us
    mul x2, other arithmetic, local(): voltage = samples.astype(jnp.float32) * 0.25 * input_gains[None, :, None]  3.28 us
  transfers between devices with their start and end apart: 1, of which 1 were waited for; matrix products, arithmetic and copies ran while one was open for 0% of the time, Pallas kernels for 0%

commit v1 on v0

v1 whole, which is shorter than its diff:
```python
import math

import numpy as np

import jax
import jax.numpy as jnp
from jax import lax
from jax.experimental import pallas as pl
from jax.experimental.pallas import tpu as pltpu
from jax.sharding import PartitionSpec as P

NFFT = 1024
TAPS = 4
SPEC = 64
CH_DEV = 4


def dft_table_np(channels):
    position = np.arange(NFFT, dtype=np.int64)
    channel = np.arange(channels, dtype=np.int64)
    phases = (position[:, None] * channel[None, :] % NFFT).astype(np.float64) * (2.0 * math.pi / NFFT)
    scaling = 0.5 / math.sqrt(NFFT)
    cosine = np.cos(phases) * scaling
    sine = np.sin(phases) * scaling
    real_rows = np.stack([cosine, -sine], axis=1)
    imag_rows = np.stack([sine, cosine], axis=1)
    table = np.stack([real_rows, imag_rows], axis=0).reshape(2, NFFT, 2 * channels)
    return jnp.asarray(table, dtype=jnp.bfloat16)


def pfb_dft_kernel(g_ref, taps_ref, s_ref, tab_ref, o_ref, acc_ref, f_ref):
    p = pl.program_id(0)
    inputs_here = s_ref.shape[1]
    scale = g_ref[...] * 0.25

    def frame(m, carry):
        total = None
        for t in range(TAPS):
            start = pl.multiple_of((m + t) * NFFT, NFFT)
            volts = s_ref[0, :, pl.ds(start, NFFT)].astype(jnp.float32) * scale
            term = volts * taps_ref[t : t + 1, :]
            total = term if total is None else total + term
        row = pl.multiple_of(m * inputs_here, inputs_here)
        f_ref[pl.ds(row, inputs_here), :] = total
        return carry

    lax.fori_loop(0, SPEC, frame, 0)
    prod = jnp.dot(
        f_ref[...].astype(jnp.bfloat16), tab_ref[0], preferred_element_type=jnp.float32
    )

    @pl.when(p == 0)
    def _():
        acc_ref[...] = prod

    @pl.when(p == 1)
    def _():
        o_ref[...] = (acc_ref[...] + prod).astype(o_ref.dtype)


def pfb_dft(samples, gains, taps, table):
    inputs_here, nsamp = samples.shape[1], samples.shape[2]
    width = table.shape[2]
    rows = SPEC * inputs_here
    return pl.pallas_call(
        pfb_dft_kernel,
        grid=(2,),
        out_shape=jax.ShapeDtypeStruct((rows, width), jnp.bfloat16),
        in_specs=[
            pl.BlockSpec((inputs_here, 1), lambda p: (0, 0)),
            pl.BlockSpec((TAPS, NFFT), lambda p: (0, 0)),
            pl.BlockSpec((1, inputs_here, nsamp), lambda p: (p, 0, 0)),
            pl.BlockSpec((1, NFFT, width), lambda p: (p, 0, 0)),
        ],
        out_specs=pl.BlockSpec((rows, width), lambda p: (0, 0)),
        scratch_shapes=[
            pltpu.VMEM((rows, width), jnp.float32),
            pltpu.VMEM((rows, NFFT), jnp.float32),
        ],
        compiler_params=pltpu.CompilerParams(vmem_limit_bytes=48 * 1024 * 1024),
    )(gains.reshape(inputs_here, 1), taps, samples, table)


def local(samples, input_gains, filter_taps):
    channels = CH_DEV * lax.axis_size("freq")
    inputs_here = samples.shape[1]
    table = dft_table_np(channels)
    flat = pfb_dft(samples, input_gains, filter_taps, table)
    spectra = flat.reshape(SPEC, inputs_here, 2, channels).transpose(3, 1, 2, 0)
    spectra = spectra.reshape(channels, inputs_here, 2 * SPEC)
    grouped = lax.all_to_all(spectra, "freq", split_axis=0, concat_axis=1, tiled=True)
    row_data = lax.all_gather(grouped, "col", axis=1, tiled=True)
    r = lax.axis_index("row")
    c = lax.axis_index("col")
    half = row_data.shape[1] // 2
    own_half = lax.dynamic_slice_in_dim(row_data, (c % 2) * half, half, 1)
    col_count = lax.axis_size("col")
    pairs = []
    for cc in range(col_count):
        rr = cc // 2
        pairs.append((rr * col_count + cc, (1 - rr) * col_count + cc))
    moved = lax.ppermute(own_half, ("row", "col"), pairs)
    column_data = jnp.where(c // 2 == r, own_half, moved)
    rotated = jnp.concatenate([-column_data[:, :, SPEC:], column_data[:, :, :SPEC]], axis=2)
    vis_real = (
        jnp.einsum("kim,kjm->kij", row_data, column_data, preferred_element_type=jnp.float32)
        * (1.0 / SPEC)
    ).astype(jnp.bfloat16)
    vis_imag = (
        jnp.einsum("kim,kjm->kij", row_data, rotated, preferred_element_type=jnp.float32)
        * (1.0 / SPEC)
    ).astype(jnp.bfloat16)
    return (vis_real, vis_imag)


def solution(mesh):
    placed = (P(None, ("row", "col", "freq"), None), P(("row", "col", "freq")), P())
    return jax.shard_map(
        local,
        mesh=mesh,
        in_specs=placed,
        out_specs=(P("freq", "row", "col"), P("freq", "row", "col")),
        check_vma=False,
    )
```

time: 105 us -> 99.3 us (0.946)
  Pallas kernels: 0 us -> 11.7 us
  other arithmetic: 9.08 us -> 1.41 us
  matrix products: 13.5 us -> 6.62 us
  waiting for transfers between devices: 35.7 us -> 32.2 us
  local copies, waits for them, and re-layouts: 9.47 us -> 7.09 us
  starting transfers between devices: 0.04 us -> 2.26 us
    all_gather x1, waiting for transfers between devices: 35.7 us -> 21.2 us  [local(): row_data = lax.all_gather(grouped, 'col', axis=1, tiled=True)]
    pallas_call x0 -> x1, Pallas kernels: none -> 11.7 us  [pfb_dft(): pl.pallas_call(pfb_dft_kernel, grid=(2,), out_shape=jax.ShapeDtypeStruct(...]
    ppermute x0 -> x1, waiting for transfers between devices: none -> 11 us  [local(): moved = lax.ppermute(own_half, ('row', 'col'), pairs)]
    slice x3 -> x0, local copies, waits for them, and re-layouts: 7.41 us -> none  [the longest x1 3.86 us: local(): vis_imag = product[:, :, width:].astype(jnp.bfloat16)]
    dot_general x2, matrix products: 13.5 us -> 6.62 us  [the longest x1 3.35 us: local(): jnp.einsum('kim,kjm->kij', row_data, rotated, preferred_element_type=jnp....]
    another operation x3 -> x0, other arithmetic: 4.31 us -> none
    unnamed x2 -> x8, local copies, waits for them, and re-layouts: 0.01 us -> 4.19 us
    mul x2 -> x0, other arithmetic: 3.28 us -> none  [local(): voltage = samples.astype(jnp.float32) * 0.25 * input_gains[None, :, None]]
  transfers between devices with their start and end apart: 1 -> 2, of which waited for: 1 -> 2; matrix products, arithmetic and copies ran while one was open for 0% -> 0% of each run, Pallas kernels for 0% -> 0%
where the time goes in v1:
time: 99.3 us; the launch traced here: 98.4 us
  waiting for transfers between devices  32.2 us (32%)
  blocking collectives  23 us (23%)
  between operations  14.1 us (14%)
  Pallas kernels  11.7 us (12%)
  local copies, waits for them, and re-layouts  7.09 us (7%)
  matrix products  6.62 us (7%)
  starting transfers between devices  2.26 us (2%)
  other arithmetic  1.41 us (1%)
    all_to_all x1, blocking collectives, local(): lax.all_to_all(spectra, 'freq', split_axis=0, concat_axis=1, tiled=True)  23 us
    all_gather x1, waiting for transfers between devices, local(): row_data = lax.all_gather(grouped, 'col', axis=1, tiled=True)  21.2 us
    pallas_call x1, Pallas kernels, pfb_dft(): pl.pallas_call(pfb_dft_kernel, grid=(2,), out_shape=jax.ShapeDtypeStruct(...  11.7 us
    ppermute x1, waiting for transfers between devices, local(): moved = lax.ppermute(own_half, ('row', 'col'), pairs)  11 us
    unnamed x8, local copies, waits for them, and re-layouts  4.19 us
    dot_general x1, matrix products, local(): jnp.einsum('kim,kjm->kij', row_data, rotated, preferred_element_type=jnp....  3.35 us
    dot_general x1, matrix products, local(): jnp.einsum('kim,kjm->kij', row_data, column_data, preferred_element_type=...  3.27 us
    ppermute x1, starting transfers between devices, local(): moved = lax.ppermute(own_half, ('row', 'col'), pairs)  2.23 us
  transfers between devices with their start and end apart: 2, of which 2 were waited for; matrix products, arithmetic and copies ran while one was open for 0% of the time, Pallas kernels for 0%

profile of v1, /device:TPU:1, one launch (start us, length us, event | category | flops | bytes accessed | tf_op | source)
XLA Modules:
  0.0 98.4 jit_solution(15636879090087894819)
XLA Ops:
  7.2 0.0 all-gather.2.cloned.1.call-start
  7.2 0.7 copy.11.g_ref
  7.9 0.0 copy-start
  7.9 2.2 %copy-done = s32[2,8,68608]{2,1,0:T(8,128)S(1)} copy-done((s32[2,8,68608]{2,1,0:T(8,128)S(1)}, s32[2,8,68608]{2,1,0:T(8,128)}, u32[]{:S(2)}) %copy-start) | copy-done | bytes 4390936
  10.2 0.0 copy-start.1
  10.2 1.2 %copy-done.1 = bf16[2,1024,256]{2,1,0:T(8,128)(2,1)S(1)} copy-done((bf16[2,1024,256]{2,1,0:T(8,128)(2,1)S(1)}, bf16[2,1024,256]{2,1,0:T(8,128)(2,1)}, u32[]{:S(2)}) %copy-start.1) | copy-done | bytes 1048600
  11.4 0.0 copy-start.2
  11.4 0.7 copy-done.2
  12.1 11.7 %shard_map.59 = bf16[512,256]{1,0:T(8,128)(2,1)S(1)} custom-call(f32[8,1]{1,0:T(8,128)S(1)} %copy.11.g_ref, f32[4,1024]{1,0:T(4,128)S(1)} %copy-done.2, s32[2,8,68608]{2,1,0:T(8,128)S(1)} %copy-done, bf16[2,1024,256]{2,1,0:T(8,128)(2,1)S(1)} %copy-done.1), custom_call_target="tpu_custom_call" | custom-call | tf_op jit(solution)/shard_map/pallas_call | solution.py:65
  23.8 0.1 copy.12
  23.9 0.2 copy.13
  24.1 23.0 %all_to_all.18 = bf16[128,8,128]{2,1,0:T(8,128)(2,1)S(1)} all-to-all(bf16[128,8,128]{2,1,0:T(8,128)(2,1)S(1)} %copy.13), channel_id=1, replica_groups=mesh['freq'=32,'row'=2,'col'=4] {'freq'}, dimensions={0} | all-to-all | bytes 524288 | tf_op jit(solution)/shard_map/all_to_all | solution.py:91
  47.1 0.7 copy.16
  47.8 0.0 all-gather.2.cloned.1.call-update
  47.9 21.2 %all-gather.2.cloned.1.call-done = bf16[4,1024,128]{2,1,0:T(8,128)(2,1)} async-done(((bf16[4,256,128]{2,1,0:T(8,128)(2,1)}), bf16[4,1024,128]{2,1,0:T(8,128)(2,1)}) %all-gather.2.cloned.1.call-update) | async-done | bytes 1048592 | tf_op jit(solution)/shard_map/all_gather | solution.py:92
  69.1 0.0 copy-start.3
  69.1 1.2 %constant_dynamic-slice_fusion = bf16[4,512,128]{2,1,0:T(8,128)(2,1)S(1)} fusion(bf16[4,1024,128]{2,1,0:T(8,128)(2,1)} %all-gather.2.cloned.1.call-done, s32[]{:T(128)S(6)} %select_n.25), kind=kLoop, calls=%fused_computation.8 | loop fusion | bytes 1048580 | tf_op jit(solution)/shard_map/dynamic_slice | solution.py:96
  70.3 2.2 %collective-permute-start = (bf16[4,512,128]{2,1,0:T(8,128)(2,1)S(1)}, bf16[4,512,128]{2,1,0:T(8,128)(2,1)S(1)}, u32[]{:S(2)}, u32[]{:S(2)}) collective-permute-start(bf16[4,512,128]{2,1,0:T(8,128)(2,1)S(1)} %constant_dynamic-slice_fusion), channel_id=1, source_target_pairs={{0,4},{1,5},{6,2},{7,3},{8,12},{9,13},{14,10},{15,11},{16,20},{17,... | collective-permute-start | bytes 1572872 | tf_op jit(solution)/shard_map/ppermute | solution.py:102
  72.5 11.0 %collective-permute-done = bf16[4,512,128]{2,1,0:T(8,128)(2,1)S(1)} collective-permute-done((bf16[4,512,128]{2,1,0:T(8,128)(2,1)S(1)}, bf16[4,512,128]{2,1,0:T(8,128)(2,1)S(1)}, u32[]{:S(2)}, u32[]{:S(2)}) %collective-permute-start) | collective-permute-done | bytes 524320 | tf_op jit(solution)/shard_map/ppermute | solution.py:102
  83.5 1.2 %broadcast_select_fusion = bf16[4,512,128]{2,1,0:T(8,128)(2,1)S(1)} fusion(bf16[4,512,128]{2,1,0:T(8,128)(2,1)S(1)} %collective-permute-done, pred[]{:T(512)S(6)} %eq.5, bf16[4,1024,128]{2,1,0:T(8,128)(2,1)} %all-gather.2.cloned.1.call-done, s32[]{:T(128)S(6)} %select_n.25), kind=kLoop, calls=%fused_computation.6 | loop fusion | flops 262144 | bytes 1572869 | tf_op jit(solution)/shard_map/jit(_where)/select_n | solution.py:103
  84.7 0.2 slice_negate_fusion
  84.9 0.0 copy-done.3
  84.9 3.3 %multiply_convert_fusion.1 = bf16[4,1024,512]{2,1,0:T(8,128)(2,1)} fusion(bf16[4,1024,128]{2,1,0:T(8,128)(2,1)S(1)} %copy-done.3, bf16[4,512,128]{2,1,0:T(8,128)(2,1)S(1)} %broadcast_select_fusion), kind=kOutput, calls=%fused_computation.1 | convolution fusion | flops 541065216 | bytes 5767168 | tf_op jit(solution)/shard_map/kim,kjm->kij/dot_general | solution.py:106
  88.2 3.4 %multiply_convert_fusion = bf16[4,1024,512]{2,1,0:T(8,128)(2,1)} fusion(bf16[4,1024,128]{2,1,0:T(8,128)(2,1)S(1)} %copy-done.3, bf16[4,512,64]{2,1,0:T(8,128)(2,1)S(1)} %get-tuple-element.3, bf16[4,512,64]{2,1,0:T(8,128)(2,1)S(1)} %get-tuple-element.2), kind=kOutput, calls=%fused_computation | convolution fusion | flops 542113792 | bytes 5767168 | tf_op jit(solution)/shard_map/kim,kjm->kij/dot_general | solution.py:110
Async XLA Ops:
  7.2 61.9 %all-gather.2.cloned.1.call-start = ((), (), s32[]{:S(2)}) async-start(), calls=%async_computation.1 | async-start | bytes 1310720 | tf_op jit(solution)/shard_map/all_gather | solution.py:92
  7.9 2.2 %copy-start = (s32[2,8,68608]{2,1,0:T(8,128)S(1)}, s32[2,8,68608]{2,1,0:T(8,128)}, u32[]{:S(2)}) copy-start(s32[2,8,68608]{2,1,0:T(8,128)} %s_ref.1) | copy-start | bytes 13172740
  10.2 1.2 %copy-start.1 = (bf16[2,1024,256]{2,1,0:T(8,128)(2,1)S(1)}, bf16[2,1024,256]{2,1,0:T(8,128)(2,1)}, u32[]{:S(2)}) copy-start(bf16[2,1024,256]{2,1,0:T(8,128)(2,1)} %constant.42.clone.tab_ref) | copy-start | bytes 3145732
  11.4 0.7 copy-start.2
  69.1 15.8 %copy-start.3 = (bf16[4,1024,128]{2,1,0:T(8,128)(2,1)S(1)}, bf16[4,1024,128]{2,1,0:T(8,128)(2,1)}, u32[]{:S(2)}) copy-start(bf16[4,1024,128]{2,1,0:T(8,128)(2,1)} %all-gather.2.cloned.1.call-done) | copy-start | bytes 3145732
  70.3 13.2 %collective-permute-start = (bf16[4,512,128]{2,1,0:T(8,128)(2,1)S(1)}, bf16[4,512,128]{2,1,0:T(8,128)(2,1)S(1)}, u32[]{:S(2)}, u32[]{:S(2)}) collective-permute-start(bf16[4,512,128]{2,1,0:T(8,128)(2,1)S(1)} %constant_dynamic-slice_fusion), channel_id=1, source_target_pairs={{0,4},{1,5},{6,2},{7,3},{8,12},{9,13},{14,10},{15,11},{16,20},{17,... | collective-permute-start | bytes 1572872 | tf_op jit(solution)/shard_map/ppermute | solution.py:102
Sparse Core Ops, SparseCore 0:
  48.0 21.0 all-gather.1

commit v2 on v1

--- a/solution.py
+++ b/solution.py
@@ -81,26 +81,177 @@
     )(gains.reshape(inputs_here, 1), taps, samples, table)
 
 
+MESH = pl.DeviceIdType.MESH
+
+
+def turn_kernel(spec_ref, row_ref, col_ref, send1, recv1, own_sem, send2, recv2, recvx, local_sem):
+    nf = spec_ref.shape[0]
+    ncol = row_ref.shape[0]
+    f = lax.axis_index("freq")
+    r = lax.axis_index("row")
+    c = lax.axis_index("col")
+    cross_c = 2 * r + c // 2
+    crossing = (c // 2) != r
+
+    barrier = pltpu.get_barrier_semaphore()
+
+    def greet_freq(d, carry):
+        pl.semaphore_signal(barrier, inc=1, device_id=((f + d) % nf, r, c), device_id_type=MESH)
+        return carry
+
+    lax.fori_loop(1, nf, greet_freq, 0)
+    for d in range(1, ncol):
+        pl.semaphore_signal(barrier, inc=1, device_id=(f, r, (c + d) % ncol), device_id_type=MESH)
+    pl.semaphore_signal(barrier, inc=1, device_id=(f, 1 - r, cross_c), device_id_type=MESH)
+
+    @pl.when(crossing)
+    def _():
+        for e in range(2):
+            pl.semaphore_signal(
+                barrier, inc=1, device_id=(f, 1 - r, 2 * (c % 2) + e), device_id_type=MESH
+            )
+
+    pl.semaphore_wait(barrier, (nf - 1) + (ncol - 1) + 1 + 2 * crossing.astype(jnp.int32))
+
+    own = pltpu.make_async_copy(spec_ref.at[f], row_ref.at[c, f], own_sem)
+    own.start()
+
+    def send_freq(d, carry):
+        dest = (f + d) % nf
+        pltpu.make_async_remote_copy(
+            src_ref=spec_ref.at[dest],
+            dst_ref=row_ref.at[c, f],
+            send_sem=send1.at[d],
+            recv_sem=recv1.at[f],
+            device_id=(dest, r, c),
+            device_id_type=MESH,
+        ).start()
+        return carry
+
+    lax.fori_loop(1, nf, send_freq, 0)
+
+    def recv_freq(d, carry):
+        src = (f + nf - d) % nf
+        pltpu.make_async_remote_copy(
+            src_ref=spec_ref.at[src],
+            dst_ref=row_ref.at[c, src],
+            send_sem=send1.at[d],
+            recv_sem=recv1.at[src],
+            device_id=(src, r, c),
+            device_id_type=MESH,
+        ).wait_recv()
+        return carry
+
+    lax.fori_loop(1, nf, recv_freq, 0)
+    own.wait()
+
+    sends2 = []
+    for d in range(1, ncol):
+        cp = pltpu.make_async_remote_copy(
+            src_ref=row_ref.at[c],
+            dst_ref=row_ref.at[c],
+            send_sem=send2.at[d],
+            recv_sem=recv2.at[c],
+            device_id=(f, r, (c + d) % ncol),
+            device_id_type=MESH,
+        )
+        cp.start()
+        sends2.append(cp)
+    cross = pltpu.make_async_remote_copy(
+        src_ref=row_ref.at[c],
+        dst_ref=col_ref.at[c % 2],
+        send_sem=send2.at[0],
+        recv_sem=recvx.at[c % 2],
+        device_id=(f, 1 - r, cross_c),
+        device_id_type=MESH,
+    )
+    cross.start()
+
+    for d in range(1, ncol):
+        src = (c + ncol - d) % ncol
+        pltpu.make_async_remote_copy(
+            src_ref=row_ref.at[src],
+            dst_ref=row_ref.at[src],
+            send_sem=send2.at[d],
+            recv_sem=recv2.at[src],
+            device_id=(f, r, src),
+            device_id_type=MESH,
+        ).wait_recv()
+
+    @pl.when(crossing)
+    def _():
+        for e in range(2):
+            pltpu.make_async_remote_copy(
+                src_ref=row_ref.at[e],
+                dst_ref=col_ref.at[e],
+                send_sem=send2.at[0],
+                recv_sem=recvx.at[e],
+                device_id=(f, 1 - r, 2 * (c % 2) + e),
+                device_id_type=MESH,
+            ).wait_recv()
+
+    @pl.when(jnp.logical_not(crossing))
+    def _():
+        half = pltpu.make_async_copy(row_ref.at[pl.ds(2 * (c % 2), 2)], col_ref, local_sem)
+        half.start()
+        half.wait()
+
+    def wait_send_freq(d, carry):
+        dest = (f + d) % nf
+        pltpu.make_async_remote_copy(
+            src_ref=spec_ref.at[dest],
+            dst_ref=row_ref.at[c, f],
+            send_sem=send1.at[d],
+            recv_sem=recv1.at[f],
+            device_id=(dest, r, c),
+            device_id_type=MESH,
+        ).wait_send()
+        return carry
+
+    lax.fori_loop(1, nf, wait_send_freq, 0)
+    for cp in sends2:
+        cp.wait_send()
+    cross.wait_send()
+
+
+def corner_turn(spec):
+    nf, rows, width = spec.shape
+    ncol = lax.axis_size("col")
+    vmem = pltpu.MemorySpace.VMEM
+    return pl.pallas_call(
+        turn_kernel,
+        out_shape=(
+            jax.ShapeDtypeStruct((ncol, nf, rows, width), spec.dtype),
+            jax.ShapeDtypeStruct((2, nf, rows, width), spec.dtype),
+        ),
+        in_specs=[pl.BlockSpec(memory_space=vmem)],
+        out_specs=(pl.BlockSpec(memory_space=vmem), pl.BlockSpec(memory_space=vmem)),
+        scratch_shapes=[
+            pltpu.SemaphoreType.DMA((nf,)),
+            pltpu.SemaphoreType.DMA((nf,)),
+            pltpu.SemaphoreType.DMA,
+            pltpu.SemaphoreType.DMA((ncol,)),
+            pltpu.SemaphoreType.DMA((ncol,)),
+            pltpu.SemaphoreType.DMA((2,)),
+            pltpu.SemaphoreType.DMA,
+        ],
+        compiler_params=pltpu.CompilerParams(collective_id=0, has_side_effects=True),
+    )(spec)
+
+
 def local(samples, input_gains, filter_taps):
-    channels = CH_DEV * lax.axis_size("freq")
+    nf = lax.axis_size("freq")
+    channels = CH_DEV * nf
     inputs_here = samples.shape[1]
     table = dft_table_np(channels)
     flat = pfb_dft(samples, input_gains, filter_taps, table)
-    spectra = flat.reshape(SPEC, inputs_here, 2, channels).transpose(3, 1, 2, 0)
-    spectra = spectra.reshape(channels, inputs_here, 2 * SPEC)
-    grouped = lax.all_to_all(spectra, "freq", split_axis=0, concat_axis=1, tiled=True)
-    row_data = lax.all_gather(grouped, "col", axis=1, tiled=True)
-    r = lax.axis_index("row")
-    c = lax.axis_index("col")
-    half = row_data.shape[1] // 2
-    own_half = lax.dynamic_slice_in_dim(row_data, (c % 2) * half, half, 1)
-    col_count = lax.axis_size("col")
-    pairs = []
-    for cc in range(col_count):
-        rr = cc // 2
-        pairs.append((rr * col_count + cc, (1 - rr) * col_count + cc))
-    moved = lax.ppermute(own_half, ("row", "col"), pairs)
-    column_data = jnp.where(c // 2 == r, own_half, moved)
+    spec = flat.reshape(SPEC, inputs_here, 2, nf, CH_DEV).transpose(3, 4, 1, 2, 0)
+    spec = spec.reshape(nf, CH_DEV * inputs_here, 2 * SPEC)
+    row_blk, col_blk = corner_turn(spec)
+    row_data = row_blk.reshape(-1, nf, CH_DEV, inputs_here, 2 * SPEC).transpose(2, 0, 1, 3, 4)
+    row_data = row_data.reshape(CH_DEV, -1, 2 * SPEC)
+    column_data = col_blk.reshape(2, nf, CH_DEV, inputs_here, 2 * SPEC).transpose(2, 0, 1, 3, 4)
+    column_data = column_data.reshape(CH_DEV, -1, 2 * SPEC)
     rotated = jnp.concatenate([-column_data[:, :, SPEC:], column_data[:, :, :SPEC]], axis=2)
     vis_real = (
         jnp.einsum("kim,kjm->kij", row_data, column_data, preferred_element_type=jnp.float32)

time: 99.3 us -> 75.7 us (0.76)
  the two profiles are of different devices: /device:TPU:1 before, /device:TPU:2 now
where the time goes in v2:
time: 75.7 us; the launch traced here: 75.3 us
  Pallas kernels  49.6 us (66%)
  local copies, waits for them, and re-layouts  18.1 us (24%)
  matrix products  6.62 us (9%)
    pallas_call x1, Pallas kernels, corner_turn(): pl.pallas_call(turn_kernel, out_shape=(jax.ShapeDtypeStruct((ncol, nf, ro...  38 us
    pallas_call x1, Pallas kernels, pfb_dft(): pl.pallas_call(pfb_dft_kernel, grid=(2,), out_shape=jax.ShapeDtypeStruct(...  11.7 us
    reshape x1, local copies, waits for them, and re-layouts, local(): flat.reshape(SPEC, inputs_here, 2, nf, CH_DEV).transpose(3, 4, 1, 2, 0)  5.9 us
    unnamed x6, local copies, waits for them, and re-layouts  4.18 us
    transpose x1, local copies, waits for them, and re-layouts, local(): flat.reshape(SPEC, inputs_here, 2, nf, CH_DEV).transpose(3, 4, 1, 2, 0)  3.58 us
    dot_general x1, matrix products, local(): jnp.einsum('kim,kjm->kij', row_data, rotated, preferred_element_type=jnp....  3.35 us
    dot_general x1, matrix products, local(): jnp.einsum('kim,kjm->kij', row_data, column_data, preferred_element_type=...  3.27 us

profile of v2, /device:TPU:2, one launch (start us, length us, event | category | flops | bytes accessed | tf_op | source)
XLA Modules:
  0.0 75.3 jit_solution(474124711442002327)
XLA Ops:
  0.6 0.7 copy.10.g_ref
  1.4 0.0 copy-start
  1.4 2.2 %copy-done = s32[2,8,68608]{2,1,0:T(8,128)S(1)} copy-done((s32[2,8,68608]{2,1,0:T(8,128)S(1)}, s32[2,8,68608]{2,1,0:T(8,128)}, u32[]{:S(2)}) %copy-start) | copy-done | bytes 4390936
  3.6 0.0 copy-start.1
  3.6 1.2 %copy-done.1 = bf16[2,1024,256]{2,1,0:T(8,128)(2,1)S(1)} copy-done((bf16[2,1024,256]{2,1,0:T(8,128)(2,1)S(1)}, bf16[2,1024,256]{2,1,0:T(8,128)(2,1)}, u32[]{:S(2)}) %copy-start.1) | copy-done | bytes 1048600
  4.8 0.0 copy-start.2
  4.8 0.7 copy-done.2
  5.5 11.7 %shard_map.59 = bf16[512,256]{1,0:T(8,128)(2,1)S(1)} custom-call(f32[8,1]{1,0:T(8,128)S(1)} %copy.10.g_ref, f32[4,1024]{1,0:T(4,128)S(1)} %copy-done.2, s32[2,8,68608]{2,1,0:T(8,128)S(1)} %copy-done, bf16[2,1024,256]{2,1,0:T(8,128)(2,1)S(1)} %copy-done.1), custom_call_target="tpu_custom_call" | custom-call | tf_op jit(solution)/shard_map/pallas_call | solution.py:65
  17.2 0.1 copy.11
  17.4 5.9 %reshape.26 = bf16[64,8,2,32,4]{1,0,4,3,2:T(8,128)(2,1)} reshape(bf16[512,256]{0,1:T(8,128)(2,1)S(1)} %copy.11) | data formatting | bytes 524288 | tf_op jit(solution)/shard_map/reshape | solution.py:248
  23.3 3.6 %copy.12 = bf16[32,4,8,2,64]{4,3,2,1,0:T(2,128)(2,1)S(1)} copy(bf16[32,4,8,2,64]{2,4,1,0,3:T(8,128)(2,1)} %bitcast.15) | data formatting | bytes 524288 | tf_op jit(solution)/shard_map/transpose | solution.py:248
  26.9 1.0 %reshape.27.spec_ref = bf16[32,32,128]{2,1,0:T(8,128)(2,1)} reshape(bf16[32,4,8,2,64]{4,3,2,1,0:T(2,128)(2,1)S(1)} %copy.12) | data formatting | bytes 524288 | tf_op jit(solution)/shard_map/reshape | solution.py:249
  27.8 38.0 %shard_map.60 = (bf16[4,32,32,128]{3,2,1,0:T(8,128)(2,1)}, bf16[2,32,32,128]{3,2,1,0:T(8,128)(2,1)}) custom-call(bf16[32,32,128]{2,1,0:T(8,128)(2,1)} %reshape.27.spec_ref), custom_call_target="tpu_custom_call" | custom-call | tf_op jit(solution)/shard_map/pallas_call | solution.py:221
  65.8 1.5 %copy.13 = bf16[4,4,32,8,128]{4,3,2,1,0:T(8,128)(2,1)S(1)} copy(bf16[4,4,32,8,128]{4,3,0,2,1:T(8,128)(2,1)} %bitcast.20) | data formatting | bytes 2097152 | tf_op jit(solution)/shard_map/transpose | solution.py:251
  67.3 1.1 %copy.14 = bf16[4,2,32,8,128]{4,3,2,1,0:T(8,128)(2,1)S(1)} copy(bf16[4,2,32,8,128]{4,3,0,2,1:T(8,128)(2,1)} %bitcast.21) | data formatting | bytes 1048576 | tf_op jit(solution)/shard_map/transpose | solution.py:253
  68.4 0.2 slice_negate_fusion
  68.7 3.4 %multiply_convert_fusion = bf16[4,1024,512]{2,1,0:T(8,128)(2,1)} fusion(bf16[4,1024,128]{2,1,0:T(8,128)(2,1)S(1)} %bitcast.16, bf16[4,512,64]{2,1,0:T(8,128)(2,1)S(1)} %get-tuple-element.7, bf16[4,512,64]{2,1,0:T(8,128)(2,1)S(1)} %get-tuple-element.6), kind=kOutput, calls=%fused_computation | convolution fusion | flops 542113792 | bytes 5767168 | tf_op jit(solution)/shard_map/kim,kjm->kij/dot_general | solution.py:261
  72.0 3.3 %multiply_convert_fusion.1 = bf16[4,1024,512]{2,1,0:T(8,128)(2,1)} fusion(bf16[4,1024,128]{2,1,0:T(8,128)(2,1)S(1)} %bitcast.17, bf16[4,512,128]{2,1,0:T(8,128)(2,1)S(1)} %bitcast.19), kind=kOutput, calls=%fused_computation.1 | convolution fusion | flops 541065216 | bytes 5767168 | tf_op jit(solution)/shard_map/kim,kjm->kij/dot_general | solution.py:257
Async XLA Ops:
  1.4 2.2 %copy-start = (s32[2,8,68608]{2,1,0:T(8,128)S(1)}, s32[2,8,68608]{2,1,0:T(8,128)}, u32[]{:S(2)}) copy-start(s32[2,8,68608]{2,1,0:T(8,128)} %s_ref.1) | copy-start | bytes 13172740
  3.6 1.2 %copy-start.1 = (bf16[2,1024,256]{2,1,0:T(8,128)(2,1)S(1)}, bf16[2,1024,256]{2,1,0:T(8,128)(2,1)}, u32[]{:S(2)}) copy-start(bf16[2,1024,256]{2,1,0:T(8,128)(2,1)} %constant.4.clone.tab_ref) | copy-start | bytes 3145732
  4.8 0.7 copy-start.2

commit v3 on v2

--- a/solution.py
+++ b/solution.py
@@ -24,61 +24,107 @@
     sine = np.sin(phases) * scaling
     real_rows = np.stack([cosine, -sine], axis=1)
     imag_rows = np.stack([sine, cosine], axis=1)
-    table = np.stack([real_rows, imag_rows], axis=0).reshape(2, NFFT, 2 * channels)
+    table = np.stack([real_rows, imag_rows], axis=0)
+    table = table.transpose(2, 3, 0, 1).reshape(2 * channels, 2 * NFFT)
     return jnp.asarray(table, dtype=jnp.bfloat16)
 
 
-def pfb_dft_kernel(g_ref, taps_ref, s_ref, tab_ref, o_ref, acc_ref, f_ref):
-    p = pl.program_id(0)
-    inputs_here = s_ref.shape[1]
-    scale = g_ref[...] * 0.25
-
-    def frame(m, carry):
-        total = None
-        for t in range(TAPS):
-            start = pl.multiple_of((m + t) * NFFT, NFFT)
-            volts = s_ref[0, :, pl.ds(start, NFFT)].astype(jnp.float32) * scale
-            term = volts * taps_ref[t : t + 1, :]
-            total = term if total is None else total + term
-        row = pl.multiple_of(m * inputs_here, inputs_here)
-        f_ref[pl.ds(row, inputs_here), :] = total
-        return carry
-
-    lax.fori_loop(0, SPEC, frame, 0)
-    prod = jnp.dot(
-        f_ref[...].astype(jnp.bfloat16), tab_ref[0], preferred_element_type=jnp.float32
-    )
-
-    @pl.when(p == 0)
-    def _():
-        acc_ref[...] = prod
-
-    @pl.when(p == 1)
-    def _():
-        o_ref[...] = (acc_ref[...] + prod).astype(o_ref.dtype)
+LANES = 128
+
+
+def pfb_dft_kernel(g_ref, taps_ref, s_hbm, tab_hbm, o_ref, sbuf, vbuf, tab_buf, f_ref, sems):
+    inputs_here, nsamp = s_hbm.shape[1], s_hbm.shape[2]
+    frames = nsamp // NFFT
+    first = SPEC // 2 + TAPS - 1
+    split = first * NFFT
+    blocks = NFFT // LANES
+    channels = tab_hbm.shape[0] // 2
+    parts = []
+    for p in range(2):
+        head = pltpu.make_async_copy(
+            s_hbm.at[p, :, pl.ds(0, split)], sbuf.at[p, :, pl.ds(0, split)], sems.at[2 * p]
+        )
+        tail = pltpu.make_async_copy(
+            s_hbm.at[p, :, pl.ds(split, nsamp - split)],
+            sbuf.at[p, :, pl.ds(split, nsamp - split)],
+            sems.at[2 * p + 1],
+        )
+        head.start()
+        tail.start()
+        parts.append((head, tail))
+    tab_cp = pltpu.make_async_copy(tab_hbm, tab_buf, sems.at[4])
+    tab_cp.start()
+
+    row = lax.broadcasted_iota(jnp.int32, (inputs_here, NFFT), 0)
+    scale = jnp.zeros((inputs_here, NFFT), jnp.float32)
+    for i in range(inputs_here):
+        scale = jnp.where(row == i, g_ref[i] * 0.25, scale)
+
+    def volts(p, lo, hi):
+        def body(j, carry):
+            start = pl.multiple_of(j * NFFT, NFFT)
+            vbuf[p, j] = sbuf[p, :, pl.ds(start, NFFT)].astype(jnp.float32) * scale
+            return carry
+
+        lax.fori_loop(lo, hi, body, 0)
+
+    def filt(p, lo, hi):
+        def body(m, carry):
+            total = vbuf[p, m] * taps_ref[0:1, :]
+            for t in range(1, TAPS):
+                total = total + vbuf[p, m + t] * taps_ref[t : t + 1, :]
+            rows = pl.ds(pl.multiple_of(m * inputs_here, inputs_here), inputs_here)
+            for b in range(blocks):
+                f_ref[p * blocks + b, rows, :] = total[:, b * LANES : (b + 1) * LANES]
+            return carry
+
+        lax.fori_loop(lo, hi, body, 0)
+
+    for p in range(2):
+        head, tail = parts[p]
+        head.wait()
+        volts(p, 0, first)
+        filt(p, 0, SPEC // 2)
+        tail.wait()
+        volts(p, first, frames)
+        filt(p, SPEC // 2, SPEC)
+
+    tab_cp.wait()
+    for i in range(inputs_here):
+        lhs = jnp.concatenate(
+            [f_ref[b, pl.ds(i, SPEC, stride=inputs_here), :] for b in range(2 * blocks)], axis=1
+        ).astype(jnp.bfloat16)
+        prod = lax.dot_general(
+            tab_buf[...], lhs, (((1,), (1,)), ((), ())), preferred_element_type=jnp.float32
+        )
+        val = jnp.concatenate([prod[:channels], prod[channels:]], axis=1)
+        o_ref[pl.ds(i, channels, stride=inputs_here), :] = val
 
 
 def pfb_dft(samples, gains, taps, table):
     inputs_here, nsamp = samples.shape[1], samples.shape[2]
-    width = table.shape[2]
-    rows = SPEC * inputs_here
+    channels = table.shape[0] // 2
+    frames = nsamp // NFFT
+    vmem = pltpu.MemorySpace.VMEM
     return pl.pallas_call(
         pfb_dft_kernel,
-        grid=(2,),
-        out_shape=jax.ShapeDtypeStruct((rows, width), jnp.bfloat16),
+        out_shape=jax.ShapeDtypeStruct((channels * inputs_here, 2 * SPEC), jnp.float32),
         in_specs=[
-            pl.BlockSpec((inputs_here, 1), lambda p: (0, 0)),
-            pl.BlockSpec((TAPS, NFFT), lambda p: (0, 0)),
-            pl.BlockSpec((1, inputs_here, nsamp), lambda p: (p, 0, 0)),
-            pl.BlockSpec((1, NFFT, width), lambda p: (p, 0, 0)),
+            pl.BlockSpec(memory_space=pltpu.MemorySpace.SMEM),
+            pl.BlockSpec(memory_space=vmem),
+            pl.BlockSpec(memory_space=pl.ANY),
+            pl.BlockSpec(memory_space=pl.ANY),
         ],
-        out_specs=pl.BlockSpec((rows, width), lambda p: (0, 0)),
+        out_specs=pl.BlockSpec(memory_space=vmem),
         scratch_shapes=[
-            pltpu.VMEM((rows, width), jnp.float32),
-            pltpu.VMEM((rows, NFFT), jnp.float32),
+            pltpu.VMEM((2, inputs_here, nsamp), jnp.int32),
+            pltpu.VMEM((2, frames, inputs_here, NFFT), jnp.float32),
+            pltpu.VMEM(table.shape, jnp.bfloat16),
+            pltpu.VMEM((2 * NFFT // LANES, SPEC * inputs_here, LANES), jnp.float32),
+            pltpu.SemaphoreType.DMA((5,)),
         ],
-        compiler_params=pltpu.CompilerParams(vmem_limit_bytes=48 * 1024 * 1024),
-    )(gains.reshape(inputs_here, 1), taps, samples, table)
+        compiler_params=pltpu.CompilerParams(vmem_limit_bytes=40 * 1024 * 1024),
+    )(gains, taps, samples, table)
 
 
 MESH = pl.DeviceIdType.MESH
@@ -245,8 +291,7 @@
     inputs_here = samples.shape[1]
     table = dft_table_np(channels)
     flat = pfb_dft(samples, input_gains, filter_taps, table)
-    spec = flat.reshape(SPEC, inputs_here, 2, nf, CH_DEV).transpose(3, 4, 1, 2, 0)
-    spec = spec.reshape(nf, CH_DEV * inputs_here, 2 * SPEC)
+    spec = flat.astype(jnp.bfloat16).reshape(nf, CH_DEV * inputs_here, 2 * SPEC)
     row_blk, col_blk = corner_turn(spec)
     row_data = row_blk.reshape(-1, nf, CH_DEV, inputs_here, 2 * SPEC).transpose(2, 0, 1, 3, 4)
     row_data = row_data.reshape(CH_DEV, -1, 2 * SPEC)

time: 75.7 us -> 61 us (0.81)
  local copies, waits for them, and re-layouts: 18.1 us -> 7.45 us
  Pallas kernels: 49.6 us -> 45 us
    reshape x3 -> x0, local copies, waits for them, and re-layouts: 7.58 us -> none  [the longest x1 5.9 us: local(): flat.reshape(SPEC, inputs_here, 2, nf, CH_DEV).transpose(3, 4, 1, 2, 0)]
    pallas_call x1, Pallas kernels: 11.7 us -> 6.99 us  [pfb_dft(): pl.pallas_call(pfb_dft_kernel, out_shape=jax.ShapeDtypeStruct((channels *...]
    transpose x1 -> x0, local copies, waits for them, and re-layouts: 3.58 us -> none  [local(): flat.reshape(SPEC, inputs_here, 2, nf, CH_DEV).transpose(3, 4, 1, 2, 0)]
    unnamed x6 -> x8, local copies, waits for them, and re-layouts: 4.18 us -> 4.83 us
where the time goes in v3:
time: 61 us; the launch traced here: 60.7 us
  Pallas kernels  45 us (74%)
  local copies, waits for them, and re-layouts  7.45 us (12%)
  matrix products  6.62 us (11%)
  other arithmetic  0.96 us (2%)
  between operations  0.68 us (1%)
    pallas_call x1, Pallas kernels, corner_turn(): pl.pallas_call(turn_kernel, out_shape=(jax.ShapeDtypeStruct((ncol, nf, ro...  38 us
    pallas_call x1, Pallas kernels, pfb_dft(): pl.pallas_call(pfb_dft_kernel, out_shape=jax.ShapeDtypeStruct((channels *...  6.99 us
    unnamed x8, local copies, waits for them, and re-layouts  4.83 us
    dot_general x1, matrix products, local(): jnp.einsum('kim,kjm->kij', row_data, rotated, preferred_element_type=jnp....  3.35 us
    dot_general x1, matrix products, local(): jnp.einsum('kim,kjm->kij', row_data, column_data, preferred_element_type=...  3.27 us
    transpose x1, local copies, waits for them, and re-layouts, local(): row_blk.reshape(-1, nf, CH_DEV, inputs_here, 2 * SPEC)  1.49 us

profile of v3, /device:TPU:2, one launch (start us, length us, event | category | flops | bytes accessed | tf_op | source)
XLA Modules:
  0.0 60.7 jit_solution(15577089524325196169)
XLA Ops:
  0.6 0.0 copy-start
  0.6 2.2 %copy-done = s32[2,8,68608]{2,1,0:T(8,128)S(1)} copy-done((s32[2,8,68608]{2,1,0:T(8,128)S(1)}, s32[2,8,68608]{2,1,0:T(8,128)}, u32[]{:S(2)}) %copy-start) | copy-done | bytes 4390936
  2.9 0.0 copy-start.1
  2.9 1.2 %copy-done.1 = bf16[256,2048]{1,0:T(8,128)(2,1)S(1)} copy-done((bf16[256,2048]{1,0:T(8,128)(2,1)S(1)}, bf16[256,2048]{1,0:T(8,128)(2,1)}, u32[]{:S(2)}) %copy-start.1) | copy-done | bytes 1048600
  4.1 0.0 copy-start.2
  4.1 0.7 %copy-done.2 = f32[4,1024]{1,0:T(4,128)S(1)} copy-done((f32[4,1024]{1,0:T(4,128)S(1)}, f32[4,1024]{1,0:T(4,128)}, u32[]{:S(2)}) %copy-start.2) | copy-done | bytes 16408
  4.8 0.0 copy-start.3
  4.8 0.7 %copy-done.3 = f32[8]{0:T(128)S(1)} copy-done((f32[8]{0:T(128)S(1)}, f32[8]{0:T(128)}, u32[]{:S(2)}) %copy-start.3) | copy-done | bytes 56
  5.5 7.0 %shard_map.59 = f32[1024,128]{1,0:T(8,128)S(1)} custom-call(f32[8]{0:T(128)S(1)} %copy-done.3, f32[4,1024]{1,0:T(4,128)S(1)} %copy-done.2, s32[2,8,68608]{2,1,0:T(8,128)S(1)} %copy-done, bf16[256,2048]{1,0:T(8,128)(2,1)S(1)} %copy-done.1), custom_call_target="tpu_custom_call" | custom-call | tf_op jit(solution)/shard_map/pallas_call | solution.py:109
  12.5 0.7 %convert_element_type.9 = bf16[1024,128]{1,0:T(8,128)(2,1)} convert(f32[1024,128]{1,0:T(8,128)S(1)} %shard_map.59) | non-fusion elementwise | flops 131072 | bytes 786432 | tf_op jit(solution)/shard_map/convert_element_type | solution.py:294
  13.2 38.0 %shard_map.60 = (bf16[4,32,32,128]{3,2,1,0:T(8,128)(2,1)}, bf16[2,32,32,128]{3,2,1,0:T(8,128)(2,1)}) custom-call(bf16[32,32,128]{2,1,0:T(8,128)(2,1)} %bitcast.16), custom_call_target="tpu_custom_call" | custom-call | tf_op jit(solution)/shard_map/pallas_call | solution.py:267
  51.2 1.5 %copy.6 = bf16[4,4,32,8,128]{4,3,2,1,0:T(8,128)(2,1)S(1)} copy(bf16[4,4,32,8,128]{4,3,0,2,1:T(8,128)(2,1)} %bitcast.17) | data formatting | bytes 2097152 | tf_op jit(solution)/shard_map/transpose | solution.py:296
  52.7 1.1 %copy.7 = bf16[4,2,32,8,128]{4,3,2,1,0:T(8,128)(2,1)S(1)} copy(bf16[4,2,32,8,128]{4,3,0,2,1:T(8,128)(2,1)} %bitcast.18) | data formatting | bytes 1048576 | tf_op jit(solution)/shard_map/transpose | solution.py:298
  53.8 0.2 slice_negate_fusion
  54.1 3.4 %multiply_convert_fusion = bf16[4,1024,512]{2,1,0:T(8,128)(2,1)} fusion(bf16[4,1024,128]{2,1,0:T(8,128)(2,1)S(1)} %bitcast.12, bf16[4,512,64]{2,1,0:T(8,128)(2,1)S(1)} %get-tuple-element.7, bf16[4,512,64]{2,1,0:T(8,128)(2,1)S(1)} %get-tuple-element.6), kind=kOutput, calls=%fused_computation | convolution fusion | flops 542113792 | bytes 5767168 | tf_op jit(solution)/shard_map/kim,kjm->kij/dot_general | solution.py:306
  57.4 3.3 %multiply_convert_fusion.1 = bf16[4,1024,512]{2,1,0:T(8,128)(2,1)} fusion(bf16[4,1024,128]{2,1,0:T(8,128)(2,1)S(1)} %bitcast.13, bf16[4,512,128]{2,1,0:T(8,128)(2,1)S(1)} %bitcast.15), kind=kOutput, calls=%fused_computation.1 | convolution fusion | flops 541065216 | bytes 5767168 | tf_op jit(solution)/shard_map/kim,kjm->kij/dot_general | solution.py:302
Async XLA Ops:
  0.6 2.2 %copy-start = (s32[2,8,68608]{2,1,0:T(8,128)S(1)}, s32[2,8,68608]{2,1,0:T(8,128)}, u32[]{:S(2)}) copy-start(s32[2,8,68608]{2,1,0:T(8,128)} %s_hbm.1) | copy-start | bytes 13172740
  2.9 1.2 %copy-start.1 = (bf16[256,2048]{1,0:T(8,128)(2,1)S(1)}, bf16[256,2048]{1,0:T(8,128)(2,1)}, u32[]{:S(2)}) copy-start(bf16[256,2048]{1,0:T(8,128)(2,1)} %constant.4.clone.tab_hbm) | copy-start | bytes 3145732
  4.1 0.7 %copy-start.2 = (f32[4,1024]{1,0:T(4,128)S(1)}, f32[4,1024]{1,0:T(4,128)}, u32[]{:S(2)}) copy-start(f32[4,1024]{1,0:T(4,128)} %taps_ref.1) | copy-start | bytes 49156
  4.8 0.7 %copy-start.3 = (f32[8]{0:T(128)S(1)}, f32[8]{0:T(128)}, u32[]{:S(2)}) copy-start(f32[8]{0:T(128)} %g_ref.1) | copy-start | bytes 100

commit v4 on v3

--- a/solution.py
+++ b/solution.py
@@ -130,14 +130,22 @@
 MESH = pl.DeviceIdType.MESH
 
 
-def turn_kernel(spec_ref, row_ref, col_ref, send1, recv1, own_sem, send2, recv2, recvx, local_sem):
+def turn_kernel(
+    spec_ref, row_ref, col_ref, send1, recv1, own_sem, sends, recva, recvb, recvc, recvd, local_sem
+):
     nf = spec_ref.shape[0]
-    ncol = row_ref.shape[0]
     f = lax.axis_index("freq")
     r = lax.axis_index("row")
     c = lax.axis_index("col")
-    cross_c = 2 * r + c // 2
-    crossing = (c // 2) != r
+    k = c % 2
+    h = c // 2
+    sib = c + 1 - 2 * k
+    cross_c = 2 * r + h
+    crossing = h != r
+    relay_target = jnp.logical_or(c == 1, c == 2)
+    fan_target = jnp.logical_not(relay_target)
+    relay_dest = 2 - k
+    relay_src = 2 * r + 2 - c
 
     barrier = pltpu.get_barrier_semaphore()
 
@@ -146,32 +154,38 @@
         return carry
 
     lax.fori_loop(1, nf, greet_freq, 0)
-    for d in range(1, ncol):
-        pl.semaphore_signal(barrier, inc=1, device_id=(f, r, (c + d) % ncol), device_id_type=MESH)
+    pl.semaphore_signal(barrier, inc=1, device_id=(f, r, sib), device_id_type=MESH)
     pl.semaphore_signal(barrier, inc=1, device_id=(f, 1 - r, cross_c), device_id_type=MESH)
 
     @pl.when(crossing)
     def _():
         for e in range(2):
-            pl.semaphore_signal(
-                barrier, inc=1, device_id=(f, 1 - r, 2 * (c % 2) + e), device_id_type=MESH
-            )
-
-    pl.semaphore_wait(barrier, (nf - 1) + (ncol - 1) + 1 + 2 * crossing.astype(jnp.int32))
+            pl.semaphore_signal(barrier, inc=1, device_id=(f, 1 - r, 2 * k + e), device_id_type=MESH)
+        pl.semaphore_signal(barrier, inc=1, device_id=(f, 1 - r, relay_dest), device_id_type=MESH)
+
+    @pl.when(relay_target)
+    def _():
+        pl.semaphore_signal(barrier, inc=1, device_id=(f, 1 - r, relay_src), device_id_type=MESH)
+
+    expected = (nf - 1) + 2 + 3 * crossing.astype(jnp.int32) + relay_target.astype(jnp.int32)
+    pl.semaphore_wait(barrier, expected)
 
     own = pltpu.make_async_copy(spec_ref.at[f], row_ref.at[c, f], own_sem)
     own.start()
 
-    def send_freq(d, carry):
+    def freq_copy(d):
         dest = (f + d) % nf
-        pltpu.make_async_remote_copy(
+        return pltpu.make_async_remote_copy(
             src_ref=spec_ref.at[dest],
             dst_ref=row_ref.at[c, f],
             send_sem=send1.at[d],
             recv_sem=recv1.at[f],
             device_id=(dest, r, c),
             device_id_type=MESH,
-        ).start()
+        )
+
+    def send_freq(d, carry):
+        freq_copy(d).start()
         return carry
 
     lax.fori_loop(1, nf, send_freq, 0)
@@ -191,38 +205,44 @@
     lax.fori_loop(1, nf, recv_freq, 0)
     own.wait()
 
-    sends2 = []
-    for d in range(1, ncol):
-        cp = pltpu.make_async_remote_copy(
-            src_ref=row_ref.at[c],
-            dst_ref=row_ref.at[c],
-            send_sem=send2.at[d],
-            recv_sem=recv2.at[c],
-            device_id=(f, r, (c + d) % ncol),
-            device_id_type=MESH,
-        )
-        cp.start()
-        sends2.append(cp)
-    cross = pltpu.make_async_remote_copy(
+    to_sib = pltpu.make_async_remote_copy(
         src_ref=row_ref.at[c],
-        dst_ref=col_ref.at[c % 2],
-        send_sem=send2.at[0],
-        recv_sem=recvx.at[c % 2],
+        dst_ref=row_ref.at[c],
+        send_sem=sends.at[0],
+        recv_sem=recva,
+        device_id=(f, r, sib),
+        device_id_type=MESH,
+    )
+    to_sib.start()
+    to_cross = pltpu.make_async_remote_copy(
+        src_ref=row_ref.at[c],
+        dst_ref=col_ref.at[k],
+        send_sem=sends.at[1],
+        recv_sem=recvb.at[k],
         device_id=(f, 1 - r, cross_c),
         device_id_type=MESH,
     )
-    cross.start()
-
-    for d in range(1, ncol):
-        src = (c + ncol - d) % ncol
-        pltpu.make_async_remote_copy(
-            src_ref=row_ref.at[src],
-            dst_ref=row_ref.at[src],
-            send_sem=send2.at[d],
-            recv_sem=recv2.at[src],
-            device_id=(f, r, src),
+    to_cross.start()
+
+    def relay_copy(e):
+        return pltpu.make_async_remote_copy(
+            src_ref=col_ref.at[e],
+            dst_ref=row_ref.at[2 * k + e],
+            send_sem=sends.at[2 + e],
+            recv_sem=recvc.at[e],
+            device_id=(f, 1 - r, relay_dest),
             device_id_type=MESH,
-        ).wait_recv()
+        )
+
+    def fan_copy(e, base):
+        return pltpu.make_async_remote_copy(
+            src_ref=row_ref.at[base + e],
+            dst_ref=row_ref.at[base + e],
+            send_sem=sends.at[4 + e],
+            recv_sem=recvd.at[e],
+            device_id=(f, r, sib),
+            device_id_type=MESH,
+        )
 
     @pl.when(crossing)
     def _():
@@ -230,34 +250,63 @@
             pltpu.make_async_remote_copy(
                 src_ref=row_ref.at[e],
                 dst_ref=col_ref.at[e],
-                send_sem=send2.at[0],
-                recv_sem=recvx.at[e],
-                device_id=(f, 1 - r, 2 * (c % 2) + e),
+                send_sem=sends.at[1],
+                recv_sem=recvb.at[e],
+                device_id=(f, 1 - r, 2 * k + e),
                 device_id_type=MESH,
             ).wait_recv()
+            relay_copy(e).start()
+
+    @pl.when(relay_target)
+    def _():
+        for e in range(2):
+            pltpu.make_async_remote_copy(
+                src_ref=col_ref.at[e],
+                dst_ref=row_ref.at[2 * (2 - c) + e],
+                send_sem=sends.at[2 + e],
+                recv_sem=recvc.at[e],
+                device_id=(f, 1 - r, relay_src),
+                device_id_type=MESH,
+            ).wait_recv()
+            fan_copy(e, 2 * (2 - c)).start()
+
+    @pl.when(fan_target)
+    def _():
+        for e in range(2):
+            fan_copy(e, 2 * (2 - sib)).wait_recv()
+
+    pltpu.make_async_remote_copy(
+        src_ref=row_ref.at[sib],
+        dst_ref=row_ref.at[sib],
+        send_sem=sends.at[0],
+        recv_sem=recva,
+        device_id=(f, r, sib),
+        device_id_type=MESH,
+    ).wait_recv()
 
     @pl.when(jnp.logical_not(crossing))
     def _():
-        half = pltpu.make_async_copy(row_ref.at[pl.ds(2 * (c % 2), 2)], col_ref, local_sem)
+        half = pltpu.make_async_copy(row_ref.at[pl.ds(2 * k, 2)], col_ref, local_sem)
         half.start()
         half.wait()
 
     def wait_send_freq(d, carry):
-        dest = (f + d) % nf
-        pltpu.make_async_remote_copy(
-            src_ref=spec_ref.at[dest],
-            dst_ref=row_ref.at[c, f],
-            send_sem=send1.at[d],
-            recv_sem=recv1.at[f],
-            device_id=(dest, r, c),
-            device_id_type=MESH,
-        ).wait_send()
+        freq_copy(d).wait_send()
         return carry
 
     lax.fori_loop(1, nf, wait_send_freq, 0)
-    for cp in sends2:
-        cp.wait_send()
-    cross.wait_send()
+    to_sib.wait_send()
+    to_cross.wait_send()
+
+    @pl.when(crossing)
+    def _():
+        for e in range(2):
+            relay_copy(e).wait_send()
+
+    @pl.when(relay_target)
+    def _():
+        for e in range(2):
+            fan_copy(e, 2 * (2 - c)).wait_send()
 
 
 def corner_turn(spec):
@@ -276,8 +325,10 @@
             pltpu.SemaphoreType.DMA((nf,)),
             pltpu.SemaphoreType.DMA((nf,)),
             pltpu.SemaphoreType.DMA,
-            pltpu.SemaphoreType.DMA((ncol,)),
-            pltpu.SemaphoreType.DMA((ncol,)),
+            pltpu.SemaphoreType.DMA((6,)),
+            pltpu.SemaphoreType.DMA,
+            pltpu.SemaphoreType.DMA((2,)),
+            pltpu.SemaphoreType.DMA((2,)),
             pltpu.SemaphoreType.DMA((2,)),
             pltpu.SemaphoreType.DMA,
         ],

time: 61 us -> 59 us (0.967)
  the two profiles are of different devices: /device:TPU:2 before, /device:TPU:1 now
where the time goes in v4:
time: 59 us; the launch traced here: 58.7 us
  Pallas kernels  43 us (73%)
  local copies, waits for them, and re-layouts  7.45 us (13%)
  matrix products  6.62 us (11%)
  other arithmetic  0.96 us (2%)
  between operations  0.68 us (1%)
    pallas_call x1, Pallas kernels, corner_turn(): pl.pallas_call(turn_kernel, out_shape=(jax.ShapeDtypeStruct((ncol, nf, ro...  36 us
    pallas_call x1, Pallas kernels, pfb_dft(): pl.pallas_call(pfb_dft_kernel, out_shape=jax.ShapeDtypeStruct((channels *...  6.99 us
    unnamed x8, local copies, waits for them, and re-layouts  4.83 us
    dot_general x1, matrix products, local(): jnp.einsum('kim,kjm->kij', row_data, rotated, preferred_element_type=jnp....  3.35 us
    dot_general x1, matrix products, local(): jnp.einsum('kim,kjm->kij', row_data, column_data, preferred_element_type=...  3.27 us
    transpose x1, local copies, waits for them, and re-layouts, local(): row_blk.reshape(-1, nf, CH_DEV, inputs_here, 2 * SPEC)  1.49 us

profile of v4, /device:TPU:1, one launch (start us, length us, event | category | flops | bytes accessed | tf_op | source)
XLA Modules:
  0.0 58.7 jit_solution(18365243395193739370)
XLA Ops:
  0.6 0.0 copy-start
  0.6 2.2 %copy-done = s32[2,8,68608]{2,1,0:T(8,128)S(1)} copy-done((s32[2,8,68608]{2,1,0:T(8,128)S(1)}, s32[2,8,68608]{2,1,0:T(8,128)}, u32[]{:S(2)}) %copy-start) | copy-done | bytes 4390936
  2.9 0.0 copy-start.1
  2.9 1.2 %copy-done.1 = bf16[256,2048]{1,0:T(8,128)(2,1)S(1)} copy-done((bf16[256,2048]{1,0:T(8,128)(2,1)S(1)}, bf16[256,2048]{1,0:T(8,128)(2,1)}, u32[]{:S(2)}) %copy-start.1) | copy-done | bytes 1048600
  4.1 0.0 copy-start.2
  4.1 0.7 %copy-done.2 = f32[4,1024]{1,0:T(4,128)S(1)} copy-done((f32[4,1024]{1,0:T(4,128)S(1)}, f32[4,1024]{1,0:T(4,128)}, u32[]{:S(2)}) %copy-start.2) | copy-done | bytes 16408
  4.8 0.0 copy-start.3
  4.8 0.7 %copy-done.3 = f32[8]{0:T(128)S(1)} copy-done((f32[8]{0:T(128)S(1)}, f32[8]{0:T(128)}, u32[]{:S(2)}) %copy-start.3) | copy-done | bytes 56
  5.5 7.0 %shard_map.59 = f32[1024,128]{1,0:T(8,128)S(1)} custom-call(f32[8]{0:T(128)S(1)} %copy-done.3, f32[4,1024]{1,0:T(4,128)S(1)} %copy-done.2, s32[2,8,68608]{2,1,0:T(8,128)S(1)} %copy-done, bf16[256,2048]{1,0:T(8,128)(2,1)S(1)} %copy-done.1), custom_call_target="tpu_custom_call" | custom-call | tf_op jit(solution)/shard_map/pallas_call | solution.py:109
  12.5 0.7 %convert_element_type.9 = bf16[1024,128]{1,0:T(8,128)(2,1)} convert(f32[1024,128]{1,0:T(8,128)S(1)} %shard_map.59) | non-fusion elementwise | flops 131072 | bytes 786432 | tf_op jit(solution)/shard_map/convert_element_type | solution.py:345
  13.2 36.0 %shard_map.60 = (bf16[4,32,32,128]{3,2,1,0:T(8,128)(2,1)}, bf16[2,32,32,128]{3,2,1,0:T(8,128)(2,1)}) custom-call(bf16[32,32,128]{2,1,0:T(8,128)(2,1)} %bitcast.16), custom_call_target="tpu_custom_call" | custom-call | tf_op jit(solution)/shard_map/pallas_call | solution.py:316
  49.2 1.5 %copy.6 = bf16[4,4,32,8,128]{4,3,2,1,0:T(8,128)(2,1)S(1)} copy(bf16[4,4,32,8,128]{4,3,0,2,1:T(8,128)(2,1)} %bitcast.17) | data formatting | bytes 2097152 | tf_op jit(solution)/shard_map/transpose | solution.py:347
  50.7 1.1 %copy.7 = bf16[4,2,32,8,128]{4,3,2,1,0:T(8,128)(2,1)S(1)} copy(bf16[4,2,32,8,128]{4,3,0,2,1:T(8,128)(2,1)} %bitcast.18) | data formatting | bytes 1048576 | tf_op jit(solution)/shard_map/transpose | solution.py:349
  51.8 0.2 slice_negate_fusion
  52.0 3.4 %multiply_convert_fusion = bf16[4,1024,512]{2,1,0:T(8,128)(2,1)} fusion(bf16[4,1024,128]{2,1,0:T(8,128)(2,1)S(1)} %bitcast.12, bf16[4,512,64]{2,1,0:T(8,128)(2,1)S(1)} %get-tuple-element.7, bf16[4,512,64]{2,1,0:T(8,128)(2,1)S(1)} %get-tuple-element.6), kind=kOutput, calls=%fused_computation | convolution fusion | flops 542113792 | bytes 5767168 | tf_op jit(solution)/shard_map/kim,kjm->kij/dot_general | solution.py:357
  55.4 3.3 %multiply_convert_fusion.1 = bf16[4,1024,512]{2,1,0:T(8,128)(2,1)} fusion(bf16[4,1024,128]{2,1,0:T(8,128)(2,1)S(1)} %bitcast.13, bf16[4,512,128]{2,1,0:T(8,128)(2,1)S(1)} %bitcast.15), kind=kOutput, calls=%fused_computation.1 | convolution fusion | flops 541065216 | bytes 5767168 | tf_op jit(solution)/shard_map/kim,kjm->kij/dot_general | solution.py:353
Async XLA Ops:
  0.6 2.2 %copy-start = (s32[2,8,68608]{2,1,0:T(8,128)S(1)}, s32[2,8,68608]{2,1,0:T(8,128)}, u32[]{:S(2)}) copy-start(s32[2,8,68608]{2,1,0:T(8,128)} %s_hbm.1) | copy-start | bytes 13172740
  2.9 1.2 %copy-start.1 = (bf16[256,2048]{1,0:T(8,128)(2,1)S(1)}, bf16[256,2048]{1,0:T(8,128)(2,1)}, u32[]{:S(2)}) copy-start(bf16[256,2048]{1,0:T(8,128)(2,1)} %constant.4.clone.tab_hbm) | copy-start | bytes 3145732
  4.1 0.7 %copy-start.2 = (f32[4,1024]{1,0:T(4,128)S(1)}, f32[4,1024]{1,0:T(4,128)}, u32[]{:S(2)}) copy-start(f32[4,1024]{1,0:T(4,128)} %taps_ref.1) | copy-start | bytes 49156
  4.8 0.7 %copy-start.3 = (f32[8]{0:T(128)S(1)}, f32[8]{0:T(128)}, u32[]{:S(2)}) copy-start(f32[8]{0:T(128)} %g_ref.1) | copy-start | bytes 100

commit v5 on v4

--- a/solution.py
+++ b/solution.py
@@ -128,10 +128,12 @@
 
 
 MESH = pl.DeviceIdType.MESH
+PIECES = 4
 
 
 def turn_kernel(
-    spec_ref, row_ref, col_ref, send1, recv1, own_sem, sends, recva, recvb, recvc, recvd, local_sem
+    spec_ref, row_ref, col_ref, send1, recv1, own_sem, senda, sendb, sendc, sendd,
+    recva, recvb, recvc, recvd, local_sem,
 ):
     nf = spec_ref.shape[0]
     f = lax.axis_index("freq")
@@ -190,99 +192,97 @@
 
     lax.fori_loop(1, nf, send_freq, 0)
 
-    def recv_freq(d, carry):
-        src = (f + nf - d) % nf
-        pltpu.make_async_remote_copy(
-            src_ref=spec_ref.at[src],
-            dst_ref=row_ref.at[c, src],
-            send_sem=send1.at[d],
-            recv_sem=recv1.at[src],
-            device_id=(src, r, c),
-            device_id_type=MESH,
-        ).wait_recv()
-        return carry
-
-    lax.fori_loop(1, nf, recv_freq, 0)
-    own.wait()
-
-    to_sib = pltpu.make_async_remote_copy(
-        src_ref=row_ref.at[c],
-        dst_ref=row_ref.at[c],
-        send_sem=sends.at[0],
-        recv_sem=recva,
-        device_id=(f, r, sib),
-        device_id_type=MESH,
-    )
-    to_sib.start()
-    to_cross = pltpu.make_async_remote_copy(
-        src_ref=row_ref.at[c],
-        dst_ref=col_ref.at[k],
-        send_sem=sends.at[1],
-        recv_sem=recvb.at[k],
-        device_id=(f, 1 - r, cross_c),
-        device_id_type=MESH,
-    )
-    to_cross.start()
-
-    def relay_copy(e):
-        return pltpu.make_async_remote_copy(
-            src_ref=col_ref.at[e],
-            dst_ref=row_ref.at[2 * k + e],
-            send_sem=sends.at[2 + e],
-            recv_sem=recvc.at[e],
-            device_id=(f, 1 - r, relay_dest),
-            device_id_type=MESH,
-        )
-
-    def fan_copy(e, base):
-        return pltpu.make_async_remote_copy(
-            src_ref=row_ref.at[base + e],
-            dst_ref=row_ref.at[base + e],
-            send_sem=sends.at[4 + e],
-            recv_sem=recvd.at[e],
+    size = nf // PIECES
+
+    def piece(q):
+        return pl.ds(q * size, size)
+
+    def sib_copy(q, slot):
+        return pltpu.make_async_remote_copy(
+            src_ref=row_ref.at[slot, piece(q)],
+            dst_ref=row_ref.at[slot, piece(q)],
+            send_sem=senda.at[q],
+            recv_sem=recva.at[q],
             device_id=(f, r, sib),
             device_id_type=MESH,
         )
 
-    @pl.when(crossing)
-    def _():
-        for e in range(2):
-            pltpu.make_async_remote_copy(
-                src_ref=row_ref.at[e],
-                dst_ref=col_ref.at[e],
-                send_sem=sends.at[1],
-                recv_sem=recvb.at[e],
-                device_id=(f, 1 - r, 2 * k + e),
-                device_id_type=MESH,
-            ).wait_recv()
-            relay_copy(e).start()
-
-    @pl.when(relay_target)
-    def _():
-        for e in range(2):
-            pltpu.make_async_remote_copy(
-                src_ref=col_ref.at[e],
-                dst_ref=row_ref.at[2 * (2 - c) + e],
-                send_sem=sends.at[2 + e],
-                recv_sem=recvc.at[e],
-                device_id=(f, 1 - r, relay_src),
-                device_id_type=MESH,
-            ).wait_recv()
-            fan_copy(e, 2 * (2 - c)).start()
+    def cross_copy(q, e, dev):
+        return pltpu.make_async_remote_copy(
+            src_ref=row_ref.at[c, piece(q)],
+            dst_ref=col_ref.at[e, piece(q)],
+            send_sem=sendb.at[q],
+            recv_sem=recvb.at[e * PIECES + q],
+            device_id=dev,
+            device_id_type=MESH,
+        )
+
+    def relay_copy(q, e, slot, dev):
+        return pltpu.make_async_remote_copy(
+            src_ref=col_ref.at[e, piece(q)],
+            dst_ref=row_ref.at[slot, piece(q)],
+            send_sem=sendc.at[e * PIECES + q],
+            recv_sem=recvc.at[e * PIECES + q],
+            device_id=dev,
+            device_id_type=MESH,
+        )
+
+    def fan_copy(q, e, base):
+        return pltpu.make_async_remote_copy(
+            src_ref=row_ref.at[base + e, piece(q)],
+            dst_ref=row_ref.at[base + e, piece(q)],
+            send_sem=sendd.at[e * PIECES + q],
+            recv_sem=recvd.at[e * PIECES + q],
+            device_id=(f, r, sib),
+            device_id_type=MESH,
+        )
+
+    for q in range(PIECES):
+
+        def recv_freq(j, carry):
+            src = q * size + j
+
+            @pl.when(src != f)
+            def _():
+                pltpu.make_async_remote_copy(
+                    src_ref=spec_ref.at[src],
+                    dst_ref=row_ref.at[c, src],
+                    send_sem=send1.at[0],
+                    recv_sem=recv1.at[src],
+                    device_id=(src, r, c),
+                    device_id_type=MESH,
+                ).wait_recv()
+
+            @pl.when(src == f)
+            def _():
+                own.wait()
+
+            return carry
+
+        lax.fori_loop(0, size, recv_freq, 0)
+        sib_copy(q, c).start()
+        cross_copy(q, k, (f, 1 - r, cross_c)).start()
+
+        @pl.when(crossing)
+        def _():
+            for e in range(2):
+                cross_copy(q, e, (f, 1 - r, 2 * k + e)).wait_recv()
+                relay_copy(q, e, 2 * k + e, (f, 1 - r, relay_dest)).start()
+
+        @pl.when(relay_target)
+        def _():
+            for e in range(2):
+                relay_copy(q, e, 2 * (2 - c) + e, (f, 1 - r, relay_src)).wait_recv()
+                fan_copy(q, e, 2 * (2 - c)).start()
 
     @pl.when(fan_target)
     def _():
-        for e in range(2):
-            fan_copy(e, 2 * (2 - sib)).wait_recv()
-
-    pltpu.make_async_remote_copy(
-        src_ref=row_ref.at[sib],
-        dst_ref=row_ref.at[sib],
-        send_sem=sends.at[0],
-        recv_sem=recva,
-        device_id=(f, r, sib),
-        device_id_type=MESH,
-    ).wait_recv()
+        for q in range(PIECES):
+            for e in range(2):
+                fan_copy(q, e, 2 * (2 - sib)).wait_recv()
+
+    for q in range(PIECES):
+        sib_copy(q, sib).wait_recv()
 
     @pl.when(jnp.logical_not(crossing))
     def _():
@@ -295,18 +295,21 @@
         return carry
 
     lax.fori_loop(1, nf, wait_send_freq, 0)
-    to_sib.wait_send()
-    to_cross.wait_send()
+    for q in range(PIECES):
+        sib_copy(q, c).wait_send()
+        cross_copy(q, k, (f, 1 - r, cross_c)).wait_send()
 
     @pl.when(crossing)
     def _():
-        for e in range(2):
-            relay_copy(e).wait_send()
+        for q in range(PIECES):
+            for e in range(2):
+                relay_copy(q, e, 2 * k + e, (f, 1 - r, relay_dest)).wait_send()
 
     @pl.when(relay_target)
     def _():
-        for e in range(2):
-            fan_copy(e, 2 * (2 - c)).wait_send()
+        for q in range(PIECES):
+            for e in range(2):
+                fan_copy(q, e, 2 * (2 - c)).wait_send()
 
 
 def corner_turn(spec):
@@ -325,11 +328,14 @@
             pltpu.SemaphoreType.DMA((nf,)),
             pltpu.SemaphoreType.DMA((nf,)),
             pltpu.SemaphoreType.DMA,
-            pltpu.SemaphoreType.DMA((6,)),
-            pltpu.SemaphoreType.DMA,
-            pltpu.SemaphoreType.DMA((2,)),
-            pltpu.SemaphoreType.DMA((2,)),
-            pltpu.SemaphoreType.DMA((2,)),
+            pltpu.SemaphoreType.DMA((PIECES,)),
+            pltpu.SemaphoreType.DMA((PIECES,)),
+            pltpu.SemaphoreType.DMA((2 * PIECES,)),
+            pltpu.SemaphoreType.DMA((2 * PIECES,)),
+            pltpu.SemaphoreType.DMA((PIECES,)),
+            pltpu.SemaphoreType.DMA((2 * PIECES,)),
+            pltpu.SemaphoreType.DMA((2 * PIECES,)),
+            pltpu.SemaphoreType.DMA((2 * PIECES,)),
             pltpu.SemaphoreType.DMA,
         ],
         compiler_params=pltpu.CompilerParams(collective_id=0, has_side_effects=True),

time: 59 us -> 70.6 us (1.20)
  Pallas kernels: 43 us -> 54.6 us
    pallas_call x1, Pallas kernels: 36 us -> 47.6 us  [corner_turn(): pl.pallas_call(turn_kernel, out_shape=(jax.ShapeDtypeStruct((ncol, nf, ro...]
where the time goes in v5:
time: 70.6 us; the launch traced here: 70.3 us
  Pallas kernels  54.6 us (77%)
  local copies, waits for them, and re-layouts  7.45 us (11%)
  matrix products  6.62 us (9%)
  other arithmetic  0.96 us (1%)
    pallas_call x1, Pallas kernels, corner_turn(): pl.pallas_call(turn_kernel, out_shape=(jax.ShapeDtypeStruct((ncol, nf, ro...  47.6 us
    pallas_call x1, Pallas kernels, pfb_dft(): pl.pallas_call(pfb_dft_kernel, out_shape=jax.ShapeDtypeStruct((channels *...  6.99 us
    unnamed x8, local copies, waits for them, and re-layouts  4.83 us
    dot_general x1, matrix products, local(): jnp.einsum('kim,kjm->kij', row_data, rotated, preferred_element_type=jnp....  3.35 us
    dot_general x1, matrix products, local(): jnp.einsum('kim,kjm->kij', row_data, column_data, preferred_element_type=...  3.27 us
    transpose x1, local copies, waits for them, and re-layouts, local(): row_blk.reshape(-1, nf, CH_DEV, inputs_here, 2 * SPEC)  1.49 us

profile of v5, /device:TPU:1, one launch (start us, length us, event | category | flops | bytes accessed | tf_op | source)
XLA Modules:
  0.0 70.3 jit_solution(553127448256044451)
XLA Ops:
  0.6 0.0 copy-start
  0.6 2.2 %copy-done = s32[2,8,68608]{2,1,0:T(8,128)S(1)} copy-done((s32[2,8,68608]{2,1,0:T(8,128)S(1)}, s32[2,8,68608]{2,1,0:T(8,128)}, u32[]{:S(2)}) %copy-start) | copy-done | bytes 4390936
  2.9 0.0 copy-start.1
  2.9 1.2 %copy-done.1 = bf16[256,2048]{1,0:T(8,128)(2,1)S(1)} copy-done((bf16[256,2048]{1,0:T(8,128)(2,1)S(1)}, bf16[256,2048]{1,0:T(8,128)(2,1)}, u32[]{:S(2)}) %copy-start.1) | copy-done | bytes 1048600
  4.1 0.0 copy-start.2
  4.1 0.7 %copy-done.2 = f32[4,1024]{1,0:T(4,128)S(1)} copy-done((f32[4,1024]{1,0:T(4,128)S(1)}, f32[4,1024]{1,0:T(4,128)}, u32[]{:S(2)}) %copy-start.2) | copy-done | bytes 16408
  4.8 0.0 copy-start.3
  4.8 0.7 copy-done.3
  5.5 7.0 %shard_map.59 = f32[1024,128]{1,0:T(8,128)S(1)} custom-call(f32[8]{0:T(128)S(1)} %copy-done.3, f32[4,1024]{1,0:T(4,128)S(1)} %copy-done.2, s32[2,8,68608]{2,1,0:T(8,128)S(1)} %copy-done, bf16[256,2048]{1,0:T(8,128)(2,1)S(1)} %copy-done.1), custom_call_target="tpu_custom_call" | custom-call | tf_op jit(solution)/shard_map/pallas_call | solution.py:109
  12.5 0.7 %convert_element_type.9 = bf16[1024,128]{1,0:T(8,128)(2,1)} convert(f32[1024,128]{1,0:T(8,128)S(1)} %shard_map.59) | non-fusion elementwise | flops 131072 | bytes 786432 | tf_op jit(solution)/shard_map/convert_element_type | solution.py:351
  13.2 47.6 %shard_map.60 = (bf16[4,32,32,128]{3,2,1,0:T(8,128)(2,1)}, bf16[2,32,32,128]{3,2,1,0:T(8,128)(2,1)}) custom-call(bf16[32,32,128]{2,1,0:T(8,128)(2,1)} %bitcast.16), custom_call_target="tpu_custom_call" | custom-call | tf_op jit(solution)/shard_map/pallas_call | solution.py:319
  60.8 1.5 %copy.6 = bf16[4,4,32,8,128]{4,3,2,1,0:T(8,128)(2,1)S(1)} copy(bf16[4,4,32,8,128]{4,3,0,2,1:T(8,128)(2,1)} %bitcast.17) | data formatting | bytes 2097152 | tf_op jit(solution)/shard_map/transpose | solution.py:353
  62.3 1.1 %copy.7 = bf16[4,2,32,8,128]{4,3,2,1,0:T(8,128)(2,1)S(1)} copy(bf16[4,2,32,8,128]{4,3,0,2,1:T(8,128)(2,1)} %bitcast.18) | data formatting | bytes 1048576 | tf_op jit(solution)/shard_map/transpose | solution.py:355
  63.4 0.2 slice_negate_fusion
  63.6 3.4 %multiply_convert_fusion = bf16[4,1024,512]{2,1,0:T(8,128)(2,1)} fusion(bf16[4,1024,128]{2,1,0:T(8,128)(2,1)S(1)} %bitcast.12, bf16[4,512,64]{2,1,0:T(8,128)(2,1)S(1)} %get-tuple-element.7, bf16[4,512,64]{2,1,0:T(8,128)(2,1)S(1)} %get-tuple-element.6), kind=kOutput, calls=%fused_computation | convolution fusion | flops 542113792 | bytes 5767168 | tf_op jit(solution)/shard_map/kim,kjm->kij/dot_general | solution.py:363
  67.0 3.3 %multiply_convert_fusion.1 = bf16[4,1024,512]{2,1,0:T(8,128)(2,1)} fusion(bf16[4,1024,128]{2,1,0:T(8,128)(2,1)S(1)} %bitcast.13, bf16[4,512,128]{2,1,0:T(8,128)(2,1)S(1)} %bitcast.15), kind=kOutput, calls=%fused_computation.1 | convolution fusion | flops 541065216 | bytes 5767168 | tf_op jit(solution)/shard_map/kim,kjm->kij/dot_general | solution.py:359
Async XLA Ops:
  0.6 2.2 %copy-start = (s32[2,8,68608]{2,1,0:T(8,128)S(1)}, s32[2,8,68608]{2,1,0:T(8,128)}, u32[]{:S(2)}) copy-start(s32[2,8,68608]{2,1,0:T(8,128)} %s_hbm.1) | copy-start | bytes 13172740
  2.9 1.2 %copy-start.1 = (bf16[256,2048]{1,0:T(8,128)(2,1)S(1)}, bf16[256,2048]{1,0:T(8,128)(2,1)}, u32[]{:S(2)}) copy-start(bf16[256,2048]{1,0:T(8,128)(2,1)} %constant.4.clone.tab_hbm) | copy-start | bytes 3145732
  4.1 0.7 %copy-start.2 = (f32[4,1024]{1,0:T(4,128)S(1)}, f32[4,1024]{1,0:T(4,128)}, u32[]{:S(2)}) copy-start(f32[4,1024]{1,0:T(4,128)} %taps_ref.1) | copy-start | bytes 49156
  4.8 0.7 copy-start.3

commit v6 on v4

--- a/solution.py
+++ b/solution.py
@@ -13,6 +13,7 @@
 TAPS = 4
 SPEC = 64
 CH_DEV = 4
+FREQ_Y = 4
 
 
 def dft_table_np(channels):
@@ -25,6 +26,9 @@
     real_rows = np.stack([cosine, -sine], axis=1)
     imag_rows = np.stack([sine, cosine], axis=1)
     table = np.stack([real_rows, imag_rows], axis=0)
+    groups = channels // CH_DEV
+    order = np.arange(channels).reshape(groups // FREQ_Y, FREQ_Y, CH_DEV).transpose(1, 0, 2).reshape(-1)
+    table = table[:, :, :, order]
     table = table.transpose(2, 3, 0, 1).reshape(2 * channels, 2 * NFFT)
     return jnp.asarray(table, dtype=jnp.bfloat16)
 
@@ -131,9 +135,10 @@
 
 
 def turn_kernel(
-    spec_ref, row_ref, col_ref, send1, recv1, own_sem, sends, recva, recvb, recvc, recvd, local_sem
+    spec_ref, row_ref, col_ref, mid_ref, send1, recv1, send2, recv2, own_sem, sends,
+    recva, recvb, recvc, recvd, local_sem,
 ):
-    nf = spec_ref.shape[0]
+    nf = spec_ref.shape[0] * spec_ref.shape[1]
     f = lax.axis_index("freq")
     r = lax.axis_index("row")
     c = lax.axis_index("col")
@@ -147,13 +152,20 @@
     relay_dest = 2 - k
     relay_src = 2 * r + 2 - c
 
+    ny = FREQ_Y
+    nz = nf // ny
+    z = f // ny
+    y = f % ny
+
     barrier = pltpu.get_barrier_semaphore()
-
-    def greet_freq(d, carry):
-        pl.semaphore_signal(barrier, inc=1, device_id=((f + d) % nf, r, c), device_id_type=MESH)
+    for d in range(1, ny):
+        pl.semaphore_signal(barrier, inc=1, device_id=(z * ny + (y + d) % ny, r, c), device_id_type=MESH)
+
+    def greet_z(d, carry):
+        pl.semaphore_signal(barrier, inc=1, device_id=(((z + d) % nz) * ny + y, r, c), device_id_type=MESH)
         return carry
 
-    lax.fori_loop(1, nf, greet_freq, 0)
+    lax.fori_loop(1, nz, greet_z, 0)
     pl.semaphore_signal(barrier, inc=1, device_id=(f, r, sib), device_id_type=MESH)
     pl.semaphore_signal(barrier, inc=1, device_id=(f, 1 - r, cross_c), device_id_type=MESH)
 
@@ -167,43 +179,71 @@
     def _():
         pl.semaphore_signal(barrier, inc=1, device_id=(f, 1 - r, relay_src), device_id_type=MESH)
 
-    expected = (nf - 1) + 2 + 3 * crossing.astype(jnp.int32) + relay_target.astype(jnp.int32)
+    expected = (ny - 1) + (nz - 1) + 2 + 3 * crossing.astype(jnp.int32) + relay_target.astype(jnp.int32)
     pl.semaphore_wait(barrier, expected)
 
-    own = pltpu.make_async_copy(spec_ref.at[f], row_ref.at[c, f], own_sem)
-    own.start()
-
-    def freq_copy(d):
-        dest = (f + d) % nf
+    own_y = pltpu.make_async_copy(spec_ref.at[y], mid_ref.at[y], own_sem.at[0])
+    own_y.start()
+
+    def y_copy(d):
+        dest = (y + d) % ny
         return pltpu.make_async_remote_copy(
             src_ref=spec_ref.at[dest],
-            dst_ref=row_ref.at[c, f],
+            dst_ref=mid_ref.at[y],
             send_sem=send1.at[d],
-            recv_sem=recv1.at[f],
-            device_id=(dest, r, c),
-            device_id_type=MESH,
-        )
-
-    def send_freq(d, carry):
-        freq_copy(d).start()
-        return carry
-
-    lax.fori_loop(1, nf, send_freq, 0)
-
-    def recv_freq(d, carry):
-        src = (f + nf - d) % nf
+            recv_sem=recv1.at[y],
+            device_id=(z * ny + dest, r, c),
+            device_id_type=MESH,
+        )
+
+    for d in range(1, ny):
+        y_copy(d).start()
+    for d in range(1, ny):
+        src = (y + ny - d) % ny
         pltpu.make_async_remote_copy(
             src_ref=spec_ref.at[src],
-            dst_ref=row_ref.at[c, src],
+            dst_ref=mid_ref.at[src],
             send_sem=send1.at[d],
             recv_sem=recv1.at[src],
-            device_id=(src, r, c),
+            device_id=(z * ny + src, r, c),
+            device_id_type=MESH,
+        ).wait_recv()
+    own_y.wait()
+
+    own_z = pltpu.make_async_copy(mid_ref.at[:, z], row_ref.at[c, pl.ds(z * ny, ny)], own_sem.at[1])
+    own_z.start()
+
+    def z_copy(d):
+        dest = (z + d) % nz
+        return pltpu.make_async_remote_copy(
+            src_ref=mid_ref.at[:, dest],
+            dst_ref=row_ref.at[c, pl.ds(z * ny, ny)],
+            send_sem=send2.at[d],
+            recv_sem=recv2.at[z],
+            device_id=(dest * ny + y, r, c),
+            device_id_type=MESH,
+        )
+
+    def send_z(d, carry):
+        z_copy(d).start()
+        return carry
+
+    lax.fori_loop(1, nz, send_z, 0)
+
+    def recv_z(d, carry):
+        src = (z + nz - d) % nz
+        pltpu.make_async_remote_copy(
+            src_ref=mid_ref.at[:, src],
+            dst_ref=row_ref.at[c, pl.ds(src * ny, ny)],
+            send_sem=send2.at[d],
+            recv_sem=recv2.at[src],
+            device_id=(src * ny + y, r, c),
             device_id_type=MESH,
         ).wait_recv()
         return carry
 
-    lax.fori_loop(1, nf, recv_freq, 0)
-    own.wait()
+    lax.fori_loop(1, nz, recv_z, 0)
+    own_z.wait()
 
     to_sib = pltpu.make_async_remote_copy(
         src_ref=row_ref.at[c],
@@ -290,11 +330,14 @@
         half.start()
         half.wait()
 
-    def wait_send_freq(d, carry):
-        freq_copy(d).wait_send()
+    for d in range(1, ny):
+        y_copy(d).wait_send()
+
+    def wait_send_z(d, carry):
+        z_copy(d).wait_send()
         return carry
 
-    lax.fori_loop(1, nf, wait_send_freq, 0)
+    lax.fori_loop(1, nz, wait_send_z, 0)
     to_sib.wait_send()
     to_cross.wait_send()
 
@@ -310,7 +353,8 @@
 
 
 def corner_turn(spec):
-    nf, rows, width = spec.shape
+    ny, nz, rows, width = spec.shape
+    nf = ny * nz
     ncol = lax.axis_size("col")
     vmem = pltpu.MemorySpace.VMEM
     return pl.pallas_call(
@@ -322,9 +366,12 @@
         in_specs=[pl.BlockSpec(memory_space=vmem)],
         out_specs=(pl.BlockSpec(memory_space=vmem), pl.BlockSpec(memory_space=vmem)),
         scratch_shapes=[
-            pltpu.SemaphoreType.DMA((nf,)),
-            pltpu.SemaphoreType.DMA((nf,)),
-            pltpu.SemaphoreType.DMA,
+            pltpu.VMEM((FREQ_Y, nf // FREQ_Y, rows, width), spec.dtype),
+            pltpu.SemaphoreType.DMA((FREQ_Y,)),
+            pltpu.SemaphoreType.DMA((FREQ_Y,)),
+            pltpu.SemaphoreType.DMA((nf // FREQ_Y,)),
+            pltpu.SemaphoreType.DMA((nf // FREQ_Y,)),
+            pltpu.SemaphoreType.DMA((2,)),
             pltpu.SemaphoreType.DMA((6,)),
             pltpu.SemaphoreType.DMA,
             pltpu.SemaphoreType.DMA((2,)),
@@ -343,7 +390,7 @@
     table = dft_table_np(channels)
     flat = pfb_dft(samples, input_gains, filter_taps, table)
     spec = flat.astype(jnp.bfloat16).reshape(nf, CH_DEV * inputs_here, 2 * SPEC)
-    row_blk, col_blk = corner_turn(spec)
+    row_blk, col_blk = corner_turn(spec.reshape(FREQ_Y, nf // FREQ_Y, *spec.shape[1:]))
     row_data = row_blk.reshape(-1, nf, CH_DEV, inputs_here, 2 * SPEC).transpose(2, 0, 1, 3, 4)
     row_data = row_data.reshape(CH_DEV, -1, 2 * SPEC)
     column_data = col_blk.reshape(2, nf, CH_DEV, inputs_here, 2 * SPEC).transpose(2, 0, 1, 3, 4)

time: 59 us -> 62.9 us (1.066)
  the two profiles are of different devices: /device:TPU:1 before, /device:TPU:7 now
where the time goes in v6:
time: 62.9 us; the launch traced here: 62.5 us
  Pallas kernels  46.8 us (74%)
  local copies, waits for them, and re-layouts  7.45 us (12%)
  matrix products  6.62 us (11%)
  other arithmetic  0.96 us (2%)
  between operations  0.68 us (1%)
    pallas_call x1, Pallas kernels, corner_turn(): pl.pallas_call(turn_kernel, out_shape=(jax.ShapeDtypeStruct((ncol, nf, ro...  39.8 us
    pallas_call x1, Pallas kernels, pfb_dft(): pl.pallas_call(pfb_dft_kernel, out_shape=jax.ShapeDtypeStruct((channels *...  6.99 us
    unnamed x8, local copies, waits for them, and re-layouts  4.83 us
    dot_general x1, matrix products, local(): jnp.einsum('kim,kjm->kij', row_data, rotated, preferred_element_type=jnp....  3.35 us
    dot_general x1, matrix products, local(): jnp.einsum('kim,kjm->kij', row_data, column_data, preferred_element_type=...  3.27 us
    transpose x1, local copies, waits for them, and re-layouts, local(): row_blk.reshape(-1, nf, CH_DEV, inputs_here, 2 * SPEC)  1.49 us

profile of v6, /device:TPU:7, one launch (start us, length us, event | category | flops | bytes accessed | tf_op | source)
XLA Modules:
  0.0 62.5 jit_solution(6516452264958524922)
XLA Ops:
  0.6 0.0 copy-start
  0.6 2.2 %copy-done = s32[2,8,68608]{2,1,0:T(8,128)S(1)} copy-done((s32[2,8,68608]{2,1,0:T(8,128)S(1)}, s32[2,8,68608]{2,1,0:T(8,128)}, u32[]{:S(2)}) %copy-start) | copy-done | bytes 4390936
  2.9 0.0 copy-start.1
  2.9 1.2 %copy-done.1 = bf16[256,2048]{1,0:T(8,128)(2,1)S(1)} copy-done((bf16[256,2048]{1,0:T(8,128)(2,1)S(1)}, bf16[256,2048]{1,0:T(8,128)(2,1)}, u32[]{:S(2)}) %copy-start.1) | copy-done | bytes 1048600
  4.1 0.0 copy-start.2
  4.1 0.7 %copy-done.2 = f32[4,1024]{1,0:T(4,128)S(1)} copy-done((f32[4,1024]{1,0:T(4,128)S(1)}, f32[4,1024]{1,0:T(4,128)}, u32[]{:S(2)}) %copy-start.2) | copy-done | bytes 16408
  4.8 0.0 copy-start.3
  4.8 0.7 %copy-done.3 = f32[8]{0:T(128)S(1)} copy-done((f32[8]{0:T(128)S(1)}, f32[8]{0:T(128)}, u32[]{:S(2)}) %copy-start.3) | copy-done | bytes 56
  5.5 7.0 %shard_map.59 = f32[1024,128]{1,0:T(8,128)S(1)} custom-call(f32[8]{0:T(128)S(1)} %copy-done.3, f32[4,1024]{1,0:T(4,128)S(1)} %copy-done.2, s32[2,8,68608]{2,1,0:T(8,128)S(1)} %copy-done, bf16[256,2048]{1,0:T(8,128)(2,1)S(1)} %copy-done.1), custom_call_target="tpu_custom_call" | custom-call | tf_op jit(solution)/shard_map/pallas_call | solution.py:113
  12.5 0.7 %convert_element_type.9 = bf16[1024,128]{1,0:T(8,128)(2,1)} convert(f32[1024,128]{1,0:T(8,128)S(1)} %shard_map.59) | non-fusion elementwise | flops 131072 | bytes 786432 | tf_op jit(solution)/shard_map/convert_element_type | solution.py:392
  13.2 39.8 %shard_map.60 = (bf16[4,32,32,128]{3,2,1,0:T(8,128)(2,1)}, bf16[2,32,32,128]{3,2,1,0:T(8,128)(2,1)}) custom-call(bf16[4,8,32,128]{3,2,1,0:T(8,128)(2,1)} %bitcast.16), custom_call_target="tpu_custom_call" | custom-call | tf_op jit(solution)/shard_map/pallas_call | solution.py:360
  53.1 1.5 %copy.6 = bf16[4,4,32,8,128]{4,3,2,1,0:T(8,128)(2,1)S(1)} copy(bf16[4,4,32,8,128]{4,3,0,2,1:T(8,128)(2,1)} %bitcast.17) | data formatting | bytes 2097152 | tf_op jit(solution)/shard_map/transpose | solution.py:394
  54.5 1.1 %copy.7 = bf16[4,2,32,8,128]{4,3,2,1,0:T(8,128)(2,1)S(1)} copy(bf16[4,2,32,8,128]{4,3,0,2,1:T(8,128)(2,1)} %bitcast.18) | data formatting | bytes 1048576 | tf_op jit(solution)/shard_map/transpose | solution.py:396
  55.7 0.2 slice_negate_fusion
  55.9 3.4 %multiply_convert_fusion = bf16[4,1024,512]{2,1,0:T(8,128)(2,1)} fusion(bf16[4,1024,128]{2,1,0:T(8,128)(2,1)S(1)} %bitcast.12, bf16[4,512,64]{2,1,0:T(8,128)(2,1)S(1)} %get-tuple-element.7, bf16[4,512,64]{2,1,0:T(8,128)(2,1)S(1)} %get-tuple-element.6), kind=kOutput, calls=%fused_computation | convolution fusion | flops 542113792 | bytes 5767168 | tf_op jit(solution)/shard_map/kim,kjm->kij/dot_general | solution.py:404
  59.3 3.3 %multiply_convert_fusion.1 = bf16[4,1024,512]{2,1,0:T(8,128)(2,1)} fusion(bf16[4,1024,128]{2,1,0:T(8,128)(2,1)S(1)} %bitcast.13, bf16[4,512,128]{2,1,0:T(8,128)(2,1)S(1)} %bitcast.15), kind=kOutput, calls=%fused_computation.1 | convolution fusion | flops 541065216 | bytes 5767168 | tf_op jit(solution)/shard_map/kim,kjm->kij/dot_general | solution.py:400
Async XLA Ops:
  0.6 2.2 %copy-start = (s32[2,8,68608]{2,1,0:T(8,128)S(1)}, s32[2,8,68608]{2,1,0:T(8,128)}, u32[]{:S(2)}) copy-start(s32[2,8,68608]{2,1,0:T(8,128)} %s_hbm.1) | copy-start | bytes 13172740
  2.9 1.2 %copy-start.1 = (bf16[256,2048]{1,0:T(8,128)(2,1)S(1)}, bf16[256,2048]{1,0:T(8,128)(2,1)}, u32[]{:S(2)}) copy-start(bf16[256,2048]{1,0:T(8,128)(2,1)} %constant.4.clone.tab_hbm) | copy-start | bytes 3145732
  4.1 0.7 %copy-start.2 = (f32[4,1024]{1,0:T(4,128)S(1)}, f32[4,1024]{1,0:T(4,128)}, u32[]{:S(2)}) copy-start(f32[4,1024]{1,0:T(4,128)} %taps_ref.1) | copy-start | bytes 49156
  4.8 0.7 %copy-start.3 = (f32[8]{0:T(128)S(1)}, f32[8]{0:T(128)}, u32[]{:S(2)}) copy-start(f32[8]{0:T(128)} %g_ref.1) | copy-start | bytes 100

commit v7 on v4

--- a/solution.py
+++ b/solution.py
@@ -32,7 +32,7 @@
 LANES = 128
 
 
-def pfb_dft_kernel(g_ref, taps_ref, s_hbm, tab_hbm, o_ref, sbuf, vbuf, tab_buf, f_ref, sems):
+def pfb_dft_kernel(g_hbm, taps_hbm, s_hbm, tab_hbm, o_ref, g_ref, taps_ref, sbuf, vbuf, tab_buf, f_ref, sems):
     inputs_here, nsamp = s_hbm.shape[1], s_hbm.shape[2]
     frames = nsamp // NFFT
     first = SPEC // 2 + TAPS - 1
@@ -54,6 +54,12 @@
         parts.append((head, tail))
     tab_cp = pltpu.make_async_copy(tab_hbm, tab_buf, sems.at[4])
     tab_cp.start()
+    g_cp = pltpu.make_async_copy(g_hbm, g_ref, sems.at[5])
+    g_cp.start()
+    taps_cp = pltpu.make_async_copy(taps_hbm, taps_ref, sems.at[6])
+    taps_cp.start()
+    g_cp.wait()
+    taps_cp.wait()
 
     row = lax.broadcasted_iota(jnp.int32, (inputs_here, NFFT), 0)
     scale = jnp.zeros((inputs_here, NFFT), jnp.float32)
@@ -109,21 +115,18 @@
     return pl.pallas_call(
         pfb_dft_kernel,
         out_shape=jax.ShapeDtypeStruct((channels * inputs_here, 2 * SPEC), jnp.float32),
-        in_specs=[
-            pl.BlockSpec(memory_space=pltpu.MemorySpace.SMEM),
-            pl.BlockSpec(memory_space=vmem),
-            pl.BlockSpec(memory_space=pl.ANY),
-            pl.BlockSpec(memory_space=pl.ANY),
-        ],
+        in_specs=[pl.BlockSpec(memory_space=pl.ANY)] * 4,
         out_specs=pl.BlockSpec(memory_space=vmem),
         scratch_shapes=[
+            pltpu.SMEM((inputs_here,), jnp.float32),
+            pltpu.VMEM((TAPS, NFFT), jnp.float32),
             pltpu.VMEM((2, inputs_here, nsamp), jnp.int32),
             pltpu.VMEM((2, frames, inputs_here, NFFT), jnp.float32),
             pltpu.VMEM(table.shape, jnp.bfloat16),
             pltpu.VMEM((2 * NFFT // LANES, SPEC * inputs_here, LANES), jnp.float32),
-            pltpu.SemaphoreType.DMA((5,)),
+            pltpu.SemaphoreType.DMA((7,)),
         ],
-        compiler_params=pltpu.CompilerParams(vmem_limit_bytes=40 * 1024 * 1024),
+        compiler_params=pltpu.CompilerParams(vmem_limit_bytes=63 * 1024 * 1024),
     )(gains, taps, samples, table)
 
 

time: 59 us -> 57 us (0.966)
  local copies, waits for them, and re-layouts: 7.45 us -> 2.62 us
  Pallas kernels: 43 us -> 44.8 us
  other arithmetic: 0.96 us -> 2 us
    unnamed x8 -> x0, local copies, waits for them, and re-layouts: 4.83 us -> none
    pallas_call x1, Pallas kernels: 6.99 us -> 8.84 us  [pfb_dft(): pl.pallas_call(pfb_dft_kernel, out_shape=jax.ShapeDtypeStruct((channels *...]
    convert_element_type x1, other arithmetic: 0.73 us -> 1.77 us  [local(): spec = flat.astype(jnp.bfloat16).reshape(nf, CH_DEV * inputs_here, 2 * SPEC)]
where the time goes in v7:
time: 57 us; the launch traced here: 56.7 us
  Pallas kernels  44.8 us (79%)
  matrix products  6.62 us (12%)
  local copies, waits for them, and re-layouts  2.62 us (5%)
  other arithmetic  2 us (4%)
  between operations  0.67 us (1%)
    pallas_call x1, Pallas kernels, corner_turn(): pl.pallas_call(turn_kernel, out_shape=(jax.ShapeDtypeStruct((ncol, nf, ro...  36 us
    pallas_call x1, Pallas kernels, pfb_dft(): pl.pallas_call(pfb_dft_kernel, out_shape=jax.ShapeDtypeStruct((channels *...  8.84 us
    dot_general x1, matrix products, local(): jnp.einsum('kim,kjm->kij', row_data, rotated, preferred_element_type=jnp....  3.35 us
    dot_general x1, matrix products, local(): jnp.einsum('kim,kjm->kij', row_data, column_data, preferred_element_type=...  3.27 us
    convert_element_type x1, other arithmetic, local(): spec = flat.astype(jnp.bfloat16).reshape(nf, CH_DEV * inputs_here, 2 * SPEC)  1.77 us
    transpose x1, local copies, waits for them, and re-layouts, local(): row_blk.reshape(-1, nf, CH_DEV, inputs_here, 2 * SPEC)  1.49 us

profile of v7, /device:TPU:1, one launch (start us, length us, event | category | flops | bytes accessed | tf_op | source)
XLA Modules:
  0.0 56.7 jit_solution(2812465705027243359)
XLA Ops:
  0.6 8.8 %shard_map.59 = f32[1024,128]{1,0:T(8,128)} custom-call(f32[8]{0:T(128)} %g_hbm.1, f32[4,1024]{1,0:T(4,128)} %taps_hbm.1, s32[2,8,68608]{2,1,0:T(8,128)} %s_hbm.1, bf16[256,2048]{1,0:T(8,128)(2,1)} %constant.4.clone.tab_hbm), custom_call_target="tpu_custom_call" | custom-call | tf_op jit(solution)/shard_map/pallas_call | solution.py:115
  9.5 1.8 %convert_element_type.9 = bf16[1024,128]{1,0:T(8,128)(2,1)} convert(f32[1024,128]{1,0:T(8,128)} %shard_map.59) | non-fusion elementwise | flops 131072 | bytes 786432 | tf_op jit(solution)/shard_map/convert_element_type | solution.py:348
  11.3 36.0 %shard_map.60 = (bf16[4,32,32,128]{3,2,1,0:T(8,128)(2,1)}, bf16[2,32,32,128]{3,2,1,0:T(8,128)(2,1)}) custom-call(bf16[32,32,128]{2,1,0:T(8,128)(2,1)} %bitcast.16), custom_call_target="tpu_custom_call" | custom-call | tf_op jit(solution)/shard_map/pallas_call | solution.py:319
  47.2 1.5 %copy.6 = bf16[4,4,32,8,128]{4,3,2,1,0:T(8,128)(2,1)S(1)} copy(bf16[4,4,32,8,128]{4,3,0,2,1:T(8,128)(2,1)} %bitcast.17) | data formatting | bytes 2097152 | tf_op jit(solution)/shard_map/transpose | solution.py:350
  48.7 1.1 %copy.7 = bf16[4,2,32,8,128]{4,3,2,1,0:T(8,128)(2,1)S(1)} copy(bf16[4,2,32,8,128]{4,3,0,2,1:T(8,128)(2,1)} %bitcast.18) | data formatting | bytes 1048576 | tf_op jit(solution)/shard_map/transpose | solution.py:352
  49.9 0.2 slice_negate_fusion
  50.1 3.4 %multiply_convert_fusion = bf16[4,1024,512]{2,1,0:T(8,128)(2,1)} fusion(bf16[4,1024,128]{2,1,0:T(8,128)(2,1)S(1)} %bitcast.12, bf16[4,512,64]{2,1,0:T(8,128)(2,1)S(1)} %get-tuple-element.7, bf16[4,512,64]{2,1,0:T(8,128)(2,1)S(1)} %get-tuple-element.6), kind=kOutput, calls=%fused_computation | convolution fusion | flops 542113792 | bytes 5767168 | tf_op jit(solution)/shard_map/kim,kjm->kij/dot_general | solution.py:360
  53.5 3.3 %multiply_convert_fusion.1 = bf16[4,1024,512]{2,1,0:T(8,128)(2,1)} fusion(bf16[4,1024,128]{2,1,0:T(8,128)(2,1)S(1)} %bitcast.13, bf16[4,512,128]{2,1,0:T(8,128)(2,1)S(1)} %bitcast.15), kind=kOutput, calls=%fused_computation.1 | convolution fusion | flops 541065216 | bytes 5767168 | tf_op jit(solution)/shard_map/kim,kjm->kij/dot_general | solution.py:356

commit v8 on v7

--- a/solution.py
+++ b/solution.py
@@ -32,7 +32,7 @@
 LANES = 128
 
 
-def pfb_dft_kernel(g_hbm, taps_hbm, s_hbm, tab_hbm, o_ref, g_ref, taps_ref, sbuf, vbuf, tab_buf, f_ref, sems):
+def pfb_dft_body(g_hbm, taps_hbm, s_hbm, tab_hbm, o_ref, g_ref, taps_ref, sbuf, vbuf, tab_buf, f_ref, sems, after_start):
     inputs_here, nsamp = s_hbm.shape[1], s_hbm.shape[2]
     frames = nsamp // NFFT
     first = SPEC // 2 + TAPS - 1
@@ -58,6 +58,7 @@
     g_cp.start()
     taps_cp = pltpu.make_async_copy(taps_hbm, taps_ref, sems.at[6])
     taps_cp.start()
+    after_start()
     g_cp.wait()
     taps_cp.wait()
 
@@ -107,34 +108,13 @@
         o_ref[pl.ds(i, channels, stride=inputs_here), :] = val
 
 
-def pfb_dft(samples, gains, taps, table):
-    inputs_here, nsamp = samples.shape[1], samples.shape[2]
-    channels = table.shape[0] // 2
-    frames = nsamp // NFFT
-    vmem = pltpu.MemorySpace.VMEM
-    return pl.pallas_call(
-        pfb_dft_kernel,
-        out_shape=jax.ShapeDtypeStruct((channels * inputs_here, 2 * SPEC), jnp.float32),
-        in_specs=[pl.BlockSpec(memory_space=pl.ANY)] * 4,
-        out_specs=pl.BlockSpec(memory_space=vmem),
-        scratch_shapes=[
-            pltpu.SMEM((inputs_here,), jnp.float32),
-            pltpu.VMEM((TAPS, NFFT), jnp.float32),
-            pltpu.VMEM((2, inputs_here, nsamp), jnp.int32),
-            pltpu.VMEM((2, frames, inputs_here, NFFT), jnp.float32),
-            pltpu.VMEM(table.shape, jnp.bfloat16),
-            pltpu.VMEM((2 * NFFT // LANES, SPEC * inputs_here, LANES), jnp.float32),
-            pltpu.SemaphoreType.DMA((7,)),
-        ],
-        compiler_params=pltpu.CompilerParams(vmem_limit_bytes=63 * 1024 * 1024),
-    )(gains, taps, samples, table)
-
-
 MESH = pl.DeviceIdType.MESH
 
 
-def turn_kernel(
-    spec_ref, row_ref, col_ref, send1, recv1, own_sem, sends, recva, recvb, recvc, recvd, local_sem
+def fused_kernel(
+    g_hbm, taps_hbm, s_hbm, tab_hbm, row_ref, col_ref,
+    g_ref, taps_ref, sbuf, vbuf, tab_buf, f_ref, o_scr, spec_ref, pfb_sems,
+    send1, recv1, own_sem, sends, recva, recvb, recvc, recvd, local_sem,
 ):
     nf = spec_ref.shape[0]
     f = lax.axis_index("freq")
@@ -150,25 +130,34 @@
     relay_dest = 2 - k
     relay_src = 2 * r + 2 - c
 
+    def greet_all():
+        barrier = pltpu.get_barrier_semaphore()
+
+        def greet_freq(d, carry):
+            pl.semaphore_signal(barrier, inc=1, device_id=((f + d) % nf, r, c), device_id_type=MESH)
+            return carry
+
+        lax.fori_loop(1, nf, greet_freq, 0)
+        pl.semaphore_signal(barrier, inc=1, device_id=(f, r, sib), device_id_type=MESH)
+        pl.semaphore_signal(barrier, inc=1, device_id=(f, 1 - r, cross_c), device_id_type=MESH)
+
+        @pl.when(crossing)
+        def _():
+            for e in range(2):
+                pl.semaphore_signal(barrier, inc=1, device_id=(f, 1 - r, 2 * k + e), device_id_type=MESH)
+            pl.semaphore_signal(barrier, inc=1, device_id=(f, 1 - r, relay_dest), device_id_type=MESH)
+
+        @pl.when(relay_target)
+        def _():
+            pl.semaphore_signal(barrier, inc=1, device_id=(f, 1 - r, relay_src), device_id_type=MESH)
+
+
     barrier = pltpu.get_barrier_semaphore()
-
-    def greet_freq(d, carry):
-        pl.semaphore_signal(barrier, inc=1, device_id=((f + d) % nf, r, c), device_id_type=MESH)
-        return carry
-
-    lax.fori_loop(1, nf, greet_freq, 0)
-    pl.semaphore_signal(barrier, inc=1, device_id=(f, r, sib), device_id_type=MESH)
-    pl.semaphore_signal(barrier, inc=1, device_id=(f, 1 - r, cross_c), device_id_type=MESH)
-
-    @pl.when(crossing)
-    def _():
-        for e in range(2):
-            pl.semaphore_signal(barrier, inc=1, device_id=(f, 1 - r, 2 * k + e), device_id_type=MESH)
-        pl.semaphore_signal(barrier, inc=1, device_id=(f, 1 - r, relay_dest), device_id_type=MESH)
-
-    @pl.when(relay_target)
-    def _():
-        pl.semaphore_signal(barrier, inc=1, device_id=(f, 1 - r, relay_src), device_id_type=MESH)
+    pfb_dft_body(
+        g_hbm, taps_hbm, s_hbm, tab_hbm, o_scr, g_ref, taps_ref, sbuf, vbuf, tab_buf, f_ref,
+        pfb_sems, greet_all,
+    )
+    spec_ref[...] = o_scr[...].astype(spec_ref.dtype).reshape(spec_ref.shape)
 
     expected = (nf - 1) + 2 + 3 * crossing.astype(jnp.int32) + relay_target.astype(jnp.int32)
     pl.semaphore_wait(barrier, expected)
@@ -312,19 +301,33 @@
             fan_copy(e, 2 * (2 - c)).wait_send()
 
 
-def corner_turn(spec):
-    nf, rows, width = spec.shape
+def fused_call(samples, gains, taps, table):
+    inputs_here, nsamp = samples.shape[1], samples.shape[2]
+    channels = table.shape[0] // 2
+    frames = nsamp // NFFT
+    nf = channels // CH_DEV
+    rows = CH_DEV * inputs_here
+    width = 2 * SPEC
     ncol = lax.axis_size("col")
     vmem = pltpu.MemorySpace.VMEM
     return pl.pallas_call(
-        turn_kernel,
+        fused_kernel,
         out_shape=(
-            jax.ShapeDtypeStruct((ncol, nf, rows, width), spec.dtype),
-            jax.ShapeDtypeStruct((2, nf, rows, width), spec.dtype),
+            jax.ShapeDtypeStruct((ncol, nf, rows, width), jnp.bfloat16),
+            jax.ShapeDtypeStruct((2, nf, rows, width), jnp.bfloat16),
         ),
-        in_specs=[pl.BlockSpec(memory_space=vmem)],
+        in_specs=[pl.BlockSpec(memory_space=pl.ANY)] * 4,
         out_specs=(pl.BlockSpec(memory_space=vmem), pl.BlockSpec(memory_space=vmem)),
         scratch_shapes=[
+            pltpu.SMEM((inputs_here,), jnp.float32),
+            pltpu.VMEM((TAPS, NFFT), jnp.float32),
+            pltpu.VMEM((2, inputs_here, nsamp), jnp.int32),
+            pltpu.VMEM((2, frames, inputs_here, NFFT), jnp.float32),
+            pltpu.VMEM(table.shape, jnp.bfloat16),
+            pltpu.VMEM((2 * NFFT // LANES, SPEC * inputs_here, LANES), jnp.float32),
+            pltpu.VMEM((channels * inputs_here, width), jnp.float32),
+            pltpu.VMEM((nf, rows, width), jnp.bfloat16),
+            pltpu.SemaphoreType.DMA((7,)),
             pltpu.SemaphoreType.DMA((nf,)),
             pltpu.SemaphoreType.DMA((nf,)),
             pltpu.SemaphoreType.DMA,
@@ -335,8 +338,10 @@
             pltpu.SemaphoreType.DMA((2,)),
             pltpu.SemaphoreType.DMA,
         ],
-        compiler_params=pltpu.CompilerParams(collective_id=0, has_side_effects=True),
-    )(spec)
+        compiler_params=pltpu.CompilerParams(
+            collective_id=0, has_side_effects=True, vmem_limit_bytes=63 * 1024 * 1024
+        ),
+    )(gains, taps, samples, table)
 
 
 def local(samples, input_gains, filter_taps):
@@ -344,9 +349,7 @@
     channels = CH_DEV * nf
     inputs_here = samples.shape[1]
     table = dft_table_np(channels)
-    flat = pfb_dft(samples, input_gains, filter_taps, table)
-    spec = flat.astype(jnp.bfloat16).reshape(nf, CH_DEV * inputs_here, 2 * SPEC)
-    row_blk, col_blk = corner_turn(spec)
+    row_blk, col_blk = fused_call(samples, input_gains, filter_taps, table)
     row_data = row_blk.reshape(-1, nf, CH_DEV, inputs_here, 2 * SPEC).transpose(2, 0, 1, 3, 4)
     row_data = row_data.reshape(CH_DEV, -1, 2 * SPEC)
     column_data = col_blk.reshape(2, nf, CH_DEV, inputs_here, 2 * SPEC).transpose(2, 0, 1, 3, 4)

time: 57 us -> 52 us (0.912)
  Pallas kernels: 44.8 us -> 41.7 us
  other arithmetic: 2 us -> 0.23 us
    pallas_call x2 -> x1, Pallas kernels: 44.8 us -> 41.7 us  [fused_call(): pl.pallas_call(fused_kernel, out_shape=(jax.ShapeDtypeStruct((ncol, nf, r...]
    convert_element_type x1 -> x0, other arithmetic: 1.77 us -> none  [local(): spec = flat.astype(jnp.bfloat16).reshape(nf, CH_DEV * inputs_here, 2 * SPEC)]
where the time goes in v8:
time: 52 us; the launch traced here: 51.8 us
  Pallas kernels  41.7 us (80%)
  matrix products  6.62 us (13%)
  local copies, waits for them, and re-layouts  2.62 us (5%)
  between operations  0.66 us (1%)
    pallas_call x1, Pallas kernels, fused_call(): pl.pallas_call(fused_kernel, out_shape=(jax.ShapeDtypeStruct((ncol, nf, r...  41.7 us
    dot_general x1, matrix products, local(): jnp.einsum('kim,kjm->kij', row_data, rotated, preferred_element_type=jnp....  3.35 us
    dot_general x1, matrix products, local(): jnp.einsum('kim,kjm->kij', row_data, column_data, preferred_element_type=...  3.27 us
    transpose x1, local copies, waits for them, and re-layouts, local(): row_blk.reshape(-1, nf, CH_DEV, inputs_here, 2 * SPEC)  1.49 us
    transpose x1, local copies, waits for them, and re-layouts, local(): col_blk.reshape(2, nf, CH_DEV, inputs_here, 2 * SPEC)  1.13 us

profile of v8, /device:TPU:1, one launch (start us, length us, event | category | flops | bytes accessed | tf_op | source)
XLA Modules:
  0.0 51.8 jit_solution(246194624712568723)
XLA Ops:
  0.6 41.7 %shard_map.59 = (bf16[4,32,32,128]{3,2,1,0:T(8,128)(2,1)}, bf16[2,32,32,128]{3,2,1,0:T(8,128)(2,1)}) custom-call(f32[8]{0:T(128)} %g_hbm.1, f32[4,1024]{1,0:T(4,128)} %taps_hbm.1, s32[2,8,68608]{2,1,0:T(8,128)} %s_hbm.1, bf16[256,2048]{1,0:T(8,128)(2,1)} %constant.4.clone.tab_hbm), custom_call_target="tpu_custom_call" | custom-call | tf_op jit(solution)/shard_map/pallas_call | solution.py:313
  42.3 1.5 %copy.6 = bf16[4,4,32,8,128]{4,3,2,1,0:T(8,128)(2,1)S(1)} copy(bf16[4,4,32,8,128]{4,3,0,2,1:T(8,128)(2,1)} %bitcast.15) | data formatting | bytes 2097152 | tf_op jit(solution)/shard_map/transpose | solution.py:353
  43.8 1.1 %copy.7 = bf16[4,2,32,8,128]{4,3,2,1,0:T(8,128)(2,1)S(1)} copy(bf16[4,2,32,8,128]{4,3,0,2,1:T(8,128)(2,1)} %bitcast.16) | data formatting | bytes 1048576 | tf_op jit(solution)/shard_map/transpose | solution.py:355
  44.9 0.2 slice_negate_fusion
  45.2 3.4 %multiply_convert_fusion = bf16[4,1024,512]{2,1,0:T(8,128)(2,1)} fusion(bf16[4,1024,128]{2,1,0:T(8,128)(2,1)S(1)} %bitcast.11, bf16[4,512,64]{2,1,0:T(8,128)(2,1)S(1)} %get-tuple-element.7, bf16[4,512,64]{2,1,0:T(8,128)(2,1)S(1)} %get-tuple-element.6), kind=kOutput, calls=%fused_computation | convolution fusion | flops 542113792 | bytes 5767168 | tf_op jit(solution)/shard_map/kim,kjm->kij/dot_general | solution.py:363
  48.5 3.3 %multiply_convert_fusion.1 = bf16[4,1024,512]{2,1,0:T(8,128)(2,1)} fusion(bf16[4,1024,128]{2,1,0:T(8,128)(2,1)S(1)} %bitcast.12, bf16[4,512,128]{2,1,0:T(8,128)(2,1)S(1)} %bitcast.14), kind=kOutput, calls=%fused_computation.1 | convolution fusion | flops 541065216 | bytes 5767168 | tf_op jit(solution)/shard_map/kim,kjm->kij/dot_general | solution.py:359

commit v9 on v8

--- a/solution.py
+++ b/solution.py
@@ -350,20 +350,56 @@
     inputs_here = samples.shape[1]
     table = dft_table_np(channels)
     row_blk, col_blk = fused_call(samples, input_gains, filter_taps, table)
-    row_data = row_blk.reshape(-1, nf, CH_DEV, inputs_here, 2 * SPEC).transpose(2, 0, 1, 3, 4)
-    row_data = row_data.reshape(CH_DEV, -1, 2 * SPEC)
-    column_data = col_blk.reshape(2, nf, CH_DEV, inputs_here, 2 * SPEC).transpose(2, 0, 1, 3, 4)
-    column_data = column_data.reshape(CH_DEV, -1, 2 * SPEC)
-    rotated = jnp.concatenate([-column_data[:, :, SPEC:], column_data[:, :, :SPEC]], axis=2)
-    vis_real = (
-        jnp.einsum("kim,kjm->kij", row_data, column_data, preferred_element_type=jnp.float32)
-        * (1.0 / SPEC)
-    ).astype(jnp.bfloat16)
-    vis_imag = (
-        jnp.einsum("kim,kjm->kij", row_data, rotated, preferred_element_type=jnp.float32)
-        * (1.0 / SPEC)
-    ).astype(jnp.bfloat16)
-    return (vis_real, vis_imag)
+    return visibilities(row_blk, col_blk)
+
+
+def vis_kernel(row_ref, col_ref, vr_ref, vi_ref, a_scr, b_scr):
+    kk = pl.program_id(0)
+    groups = row_ref.shape[2] // CH_DEV
+
+    @pl.when(kk == 0)
+    def _():
+        rows = row_ref[...].astype(jnp.float32)
+        cols = col_ref[...].astype(jnp.float32)
+        for j in range(CH_DEV):
+            a = rows[:, :, j * groups : (j + 1) * groups, :]
+            a_scr[j] = a.reshape(-1, a.shape[-1]).astype(a_scr.dtype)
+            b = cols[:, :, j * groups : (j + 1) * groups, :]
+            b = b.reshape(-1, b.shape[-1])
+            b_scr[j, 0] = b.astype(b_scr.dtype)
+            b_scr[j, 1] = jnp.concatenate([-b[:, SPEC:], b[:, :SPEC]], axis=1).astype(b_scr.dtype)
+
+    a = a_scr[kk]
+    dims = (((1,), (1,)), ((), ()))
+    vr = lax.dot_general(a, b_scr[kk, 0], dims, preferred_element_type=jnp.float32)
+    vr_ref[0] = (vr * (1.0 / SPEC)).astype(vr_ref.dtype)
+    vi = lax.dot_general(a, b_scr[kk, 1], dims, preferred_element_type=jnp.float32)
+    vi_ref[0] = (vi * (1.0 / SPEC)).astype(vi_ref.dtype)
+
+
+def visibilities(row_blk, col_blk):
+    nrow = row_blk.shape[0] * row_blk.shape[1] * row_blk.shape[2] // CH_DEV
+    ncolumn = col_blk.shape[0] * col_blk.shape[1] * col_blk.shape[2] // CH_DEV
+    width = row_blk.shape[3]
+    out = jax.ShapeDtypeStruct((CH_DEV, nrow, ncolumn), jnp.bfloat16)
+    return pl.pallas_call(
+        vis_kernel,
+        grid=(CH_DEV,),
+        out_shape=(out, out),
+        in_specs=[
+            pl.BlockSpec(row_blk.shape, lambda k: (0, 0, 0, 0)),
+            pl.BlockSpec(col_blk.shape, lambda k: (0, 0, 0, 0)),
+        ],
+        out_specs=(
+            pl.BlockSpec((1, nrow, ncolumn), lambda k: (k, 0, 0)),
+            pl.BlockSpec((1, nrow, ncolumn), lambda k: (k, 0, 0)),
+        ),
+        scratch_shapes=[
+            pltpu.VMEM((CH_DEV, nrow, width), jnp.bfloat16),
+            pltpu.VMEM((CH_DEV, 2, ncolumn, width), jnp.bfloat16),
+        ],
+        compiler_params=pltpu.CompilerParams(vmem_limit_bytes=48 * 1024 * 1024),
+    )(row_blk, col_blk)
 
 
 def solution(mesh):

time: 52 us -> 49.5 us (0.952)
  matrix products: 6.62 us -> 0 us
  Pallas kernels: 41.7 us -> 46.4 us
    dot_general x2 -> x0, matrix products: 6.62 us -> none  [the longest x1 3.35 us: local(): jnp.einsum('kim,kjm->kij', row_data, rotated, preferred_element_type=jnp....]
    pallas_call x0 -> x1, Pallas kernels: none -> 4.71 us  [visibilities(): pl.pallas_call(vis_kernel, grid=(CH_DEV,), out_shape=(out, out), in_specs...]
    transpose x2 -> x0, local copies, waits for them, and re-layouts: 2.62 us -> none  [the longest x1 1.49 us: local(): row_blk.reshape(-1, nf, CH_DEV, inputs_here, 2 * SPEC)]
    unnamed x0 -> x4, local copies, waits for them, and re-layouts: none -> 2.26 us
where the time goes in v9:
time: 49.5 us; the launch traced here: 49.3 us
  Pallas kernels  46.4 us (94%)
  local copies, waits for them, and re-layouts  2.26 us (5%)
  between operations  0.65 us (1%)
    pallas_call x1, Pallas kernels, fused_call(): pl.pallas_call(fused_kernel, out_shape=(jax.ShapeDtypeStruct((ncol, nf, r...  41.7 us
    pallas_call x1, Pallas kernels, visibilities(): pl.pallas_call(vis_kernel, grid=(CH_DEV,), out_shape=(out, out), in_specs...  4.71 us
    unnamed x4, local copies, waits for them, and re-layouts  2.26 us

profile of v9, /device:TPU:1, one launch (start us, length us, event | category | flops | bytes accessed | tf_op | source)
XLA Modules:
  0.0 49.3 jit_solution(15761839053051622334)
XLA Ops:
  0.6 41.7 %shard_map.59 = (bf16[4,32,32,128]{3,2,1,0:T(8,128)(2,1)}, bf16[2,32,32,128]{3,2,1,0:T(8,128)(2,1)}) custom-call(f32[8]{0:T(128)} %g_hbm.1, f32[4,1024]{1,0:T(4,128)} %taps_hbm.1, s32[2,8,68608]{2,1,0:T(8,128)} %s_hbm.1, bf16[256,2048]{1,0:T(8,128)(2,1)} %constant.2.clone.tab_hbm), custom_call_target="tpu_custom_call" | custom-call | tf_op jit(solution)/shard_map/pallas_call | solution.py:313
  42.3 0.0 copy-start
  42.3 1.2 %copy-done = bf16[4,32,32,128]{3,2,1,0:T(8,128)(2,1)S(1)} copy-done((bf16[4,32,32,128]{3,2,1,0:T(8,128)(2,1)S(1)}, bf16[4,32,32,128]{3,2,1,0:T(8,128)(2,1)}, u32[]{:S(2)}) %copy-start) | copy-done | bytes 1048600
  43.6 0.0 copy-start.1
  43.6 1.0 %copy-done.1 = bf16[2,32,32,128]{3,2,1,0:T(8,128)(2,1)S(1)} copy-done((bf16[2,32,32,128]{3,2,1,0:T(8,128)(2,1)S(1)}, bf16[2,32,32,128]{3,2,1,0:T(8,128)(2,1)}, u32[]{:S(2)}) %copy-start.1) | copy-done | bytes 524312
  44.6 4.7 %shard_map.60 = (bf16[4,1024,512]{2,1,0:T(8,128)(2,1)}, bf16[4,1024,512]{2,1,0:T(8,128)(2,1)}) custom-call(bf16[4,32,32,128]{3,2,1,0:T(8,128)(2,1)S(1)} %copy-done, bf16[2,32,32,128]{3,2,1,0:T(8,128)(2,1)S(1)} %copy-done.1), custom_call_target="tpu_custom_call" | custom-call | tf_op jit(solution)/shard_map/pallas_call | solution.py:385
Async XLA Ops:
  42.3 1.2 %copy-start = (bf16[4,32,32,128]{3,2,1,0:T(8,128)(2,1)S(1)}, bf16[4,32,32,128]{3,2,1,0:T(8,128)(2,1)}, u32[]{:S(2)}) copy-start(bf16[4,32,32,128]{3,2,1,0:T(8,128)(2,1)} %get-tuple-element.4.row_ref) | copy-start | bytes 3145732
  43.6 1.0 %copy-start.1 = (bf16[2,32,32,128]{3,2,1,0:T(8,128)(2,1)S(1)}, bf16[2,32,32,128]{3,2,1,0:T(8,128)(2,1)}, u32[]{:S(2)}) copy-start(bf16[2,32,32,128]{3,2,1,0:T(8,128)(2,1)} %get-tuple-element.5.col_ref) | copy-start | bytes 1572868

commit v10 on v9

--- a/solution.py
+++ b/solution.py
@@ -398,7 +398,7 @@
             pltpu.VMEM((CH_DEV, nrow, width), jnp.bfloat16),
             pltpu.VMEM((CH_DEV, 2, ncolumn, width), jnp.bfloat16),
         ],
-        compiler_params=pltpu.CompilerParams(vmem_limit_bytes=48 * 1024 * 1024),
+        compiler_params=pltpu.CompilerParams(vmem_limit_bytes=63 * 1024 * 1024),
     )(row_blk, col_blk)
 
 

time: 49.5 us -> 48.5 us (0.980)
  local copies, waits for them, and re-layouts: 2.26 us -> 0 us
  Pallas kernels: 46.4 us -> 47.7 us
    unnamed x4 -> x0, local copies, waits for them, and re-layouts: 2.26 us -> none
    pallas_call x1, Pallas kernels: 4.71 us -> 6.1 us  [visibilities(): pl.pallas_call(vis_kernel, grid=(CH_DEV,), out_shape=(out, out), in_specs...]
where the time goes in v10:
time: 48.5 us; the launch traced here: 48.4 us
  Pallas kernels  47.7 us (98%)
  between operations  0.64 us (1%)
    pallas_call x1, Pallas kernels, fused_call(): pl.pallas_call(fused_kernel, out_shape=(jax.ShapeDtypeStruct((ncol, nf, r...  41.6 us
    pallas_call x1, Pallas kernels, visibilities(): pl.pallas_call(vis_kernel, grid=(CH_DEV,), out_shape=(out, out), in_specs...  6.1 us

profile of v10, /device:TPU:1, one launch (start us, length us, event | category | flops | bytes accessed | tf_op | source)
XLA Modules:
  0.0 48.4 jit_solution(3056260591920992769)
XLA Ops:
  0.6 41.6 %shard_map.59 = (bf16[4,32,32,128]{3,2,1,0:T(8,128)(2,1)}, bf16[2,32,32,128]{3,2,1,0:T(8,128)(2,1)}) custom-call(f32[8]{0:T(128)} %g_hbm.1, f32[4,1024]{1,0:T(4,128)} %taps_hbm.1, s32[2,8,68608]{2,1,0:T(8,128)} %s_hbm.1, bf16[256,2048]{1,0:T(8,128)(2,1)} %constant.2.clone.tab_hbm), custom_call_target="tpu_custom_call" | custom-call | tf_op jit(solution)/shard_map/pallas_call | solution.py:313
  42.3 6.1 %shard_map.60 = (bf16[4,1024,512]{2,1,0:T(8,128)(2,1)}, bf16[4,1024,512]{2,1,0:T(8,128)(2,1)}) custom-call(bf16[4,32,32,128]{3,2,1,0:T(8,128)(2,1)} %get-tuple-element.4.row_ref, bf16[2,32,32,128]{3,2,1,0:T(8,128)(2,1)} %get-tuple-element.5.col_ref), custom_call_target="tpu_custom_call" | custom-call | tf_op jit(solution)/shard_map/pallas_call | solution.py:385

commit v11 on v10

--- a/solution.py
+++ b/solution.py
@@ -113,8 +113,8 @@
 
 def fused_kernel(
     g_hbm, taps_hbm, s_hbm, tab_hbm, row_ref, col_ref,
-    g_ref, taps_ref, sbuf, vbuf, tab_buf, f_ref, o_scr, spec_ref, pfb_sems,
-    send1, recv1, own_sem, sends, recva, recvb, recvc, recvd, local_sem,
+    g_ref, taps_ref, sbuf, vbuf, tab_buf, f_ref, o_scr, spec_ref, relay_buf, pfb_sems,
+    send1, recv1, own_sem, sends, recva, recvb, recvc, recvd, recve, recvf, local_sem,
 ):
     nf = spec_ref.shape[0]
     f = lax.axis_index("freq")
@@ -129,6 +129,14 @@
     fan_target = jnp.logical_not(relay_target)
     relay_dest = 2 - k
     relay_src = 2 * r + 2 - c
+    side_source = k == 1
+    side_relay = jnp.logical_not(crossing)
+    side_target = fan_target
+    side_dest = 2 * (1 - r) + h
+    side_from = 2 * k + 1
+    side_to = 3 - 3 * k
+    side_target_src = 2 * (1 - r) + 1 - h
+    base = 2 * (1 - h)
 
     def greet_all():
         barrier = pltpu.get_barrier_semaphore()
@@ -150,6 +158,19 @@
         @pl.when(relay_target)
         def _():
             pl.semaphore_signal(barrier, inc=1, device_id=(f, 1 - r, relay_src), device_id_type=MESH)
+
+        @pl.when(side_source)
+        def _():
+            pl.semaphore_signal(barrier, inc=1, device_id=(f, 1 - r, side_dest), device_id_type=MESH)
+
+        @pl.when(side_relay)
+        def _():
+            pl.semaphore_signal(barrier, inc=1, device_id=(f, 1 - r, side_from), device_id_type=MESH)
+            pl.semaphore_signal(barrier, inc=1, device_id=(f, 1 - r, side_to), device_id_type=MESH)
+
+        @pl.when(side_target)
+        def _():
+            pl.semaphore_signal(barrier, inc=1, device_id=(f, 1 - r, side_target_src), device_id_type=MESH)
 
 
     barrier = pltpu.get_barrier_semaphore()
@@ -159,7 +180,11 @@
     )
     spec_ref[...] = o_scr[...].astype(spec_ref.dtype).reshape(spec_ref.shape)
 
-    expected = (nf - 1) + 2 + 3 * crossing.astype(jnp.int32) + relay_target.astype(jnp.int32)
+    expected = (
+        (nf - 1) + 2 + 3 * crossing.astype(jnp.int32) + relay_target.astype(jnp.int32)
+        + side_source.astype(jnp.int32) + 2 * side_relay.astype(jnp.int32)
+        + side_target.astype(jnp.int32)
+    )
     pl.semaphore_wait(barrier, expected)
 
     own = pltpu.make_async_copy(spec_ref.at[f], row_ref.at[c, f], own_sem)
@@ -216,56 +241,100 @@
     )
     to_cross.start()
 
-    def relay_copy(e):
+    def side_copy():
         return pltpu.make_async_remote_copy(
-            src_ref=col_ref.at[e],
-            dst_ref=row_ref.at[2 * k + e],
-            send_sem=sends.at[2 + e],
-            recv_sem=recvc.at[e],
+            src_ref=row_ref.at[c],
+            dst_ref=relay_buf,
+            send_sem=sends.at[2],
+            recv_sem=recve,
+            device_id=(f, 1 - r, side_dest),
+            device_id_type=MESH,
+        )
+
+    def relay_copy():
+        return pltpu.make_async_remote_copy(
+            src_ref=col_ref.at[0],
+            dst_ref=row_ref.at[2 * k],
+            send_sem=sends.at[3],
+            recv_sem=recvc,
             device_id=(f, 1 - r, relay_dest),
             device_id_type=MESH,
         )
 
-    def fan_copy(e, base):
+    def side_relay_copy():
         return pltpu.make_async_remote_copy(
-            src_ref=row_ref.at[base + e],
-            dst_ref=row_ref.at[base + e],
-            send_sem=sends.at[4 + e],
-            recv_sem=recvd.at[e],
+            src_ref=relay_buf,
+            dst_ref=row_ref.at[2 * k + 1],
+            send_sem=sends.at[4],
+            recv_sem=recvf,
+            device_id=(f, 1 - r, side_to),
+            device_id_type=MESH,
+        )
+
+    def fan_copy(slot):
+        return pltpu.make_async_remote_copy(
+            src_ref=row_ref.at[slot],
+            dst_ref=row_ref.at[slot],
+            send_sem=sends.at[5],
+            recv_sem=recvd,
             device_id=(f, r, sib),
             device_id_type=MESH,
         )
 
+    mine = jnp.where(relay_target, 0, 1)
+
+    @pl.when(side_source)
+    def _():
+        side_copy().start()
+
     @pl.when(crossing)
     def _():
-        for e in range(2):
-            pltpu.make_async_remote_copy(
-                src_ref=row_ref.at[e],
-                dst_ref=col_ref.at[e],
-                send_sem=sends.at[1],
-                recv_sem=recvb.at[e],
-                device_id=(f, 1 - r, 2 * k + e),
-                device_id_type=MESH,
-            ).wait_recv()
-            relay_copy(e).start()
+        pltpu.make_async_remote_copy(
+            src_ref=row_ref.at[0],
+            dst_ref=col_ref.at[0],
+            send_sem=sends.at[1],
+            recv_sem=recvb.at[0],
+            device_id=(f, 1 - r, 2 * k),
+            device_id_type=MESH,
+        ).wait_recv()
+        relay_copy().start()
+
+    @pl.when(side_relay)
+    def _():
+        pltpu.make_async_remote_copy(
+            src_ref=row_ref.at[c],
+            dst_ref=relay_buf,
+            send_sem=sends.at[2],
+            recv_sem=recve,
+            device_id=(f, 1 - r, side_from),
+            device_id_type=MESH,
+        ).wait_recv()
+        side_relay_copy().start()
 
     @pl.when(relay_target)
     def _():
-        for e in range(2):
-            pltpu.make_async_remote_copy(
-                src_ref=col_ref.at[e],
-                dst_ref=row_ref.at[2 * (2 - c) + e],
-                send_sem=sends.at[2 + e],
-                recv_sem=recvc.at[e],
-                device_id=(f, 1 - r, relay_src),
-                device_id_type=MESH,
-            ).wait_recv()
-            fan_copy(e, 2 * (2 - c)).start()
-
-    @pl.when(fan_target)
-    def _():
-        for e in range(2):
-            fan_copy(e, 2 * (2 - sib)).wait_recv()
+        pltpu.make_async_remote_copy(
+            src_ref=col_ref.at[0],
+            dst_ref=row_ref.at[base],
+            send_sem=sends.at[3],
+            recv_sem=recvc,
+            device_id=(f, 1 - r, relay_src),
+            device_id_type=MESH,
+        ).wait_recv()
+
+    @pl.when(side_target)
+    def _():
+        pltpu.make_async_remote_copy(
+            src_ref=relay_buf,
+            dst_ref=row_ref.at[base + 1],
+            send_sem=sends.at[4],
+            recv_sem=recvf,
+            device_id=(f, 1 - r, side_target_src),
+            device_id_type=MESH,
+        ).wait_recv()
+
+    fan_copy(base + mine).start()
+    fan_copy(base + 1 - mine).wait_recv()
 
     pltpu.make_async_remote_copy(
         src_ref=row_ref.at[sib],
@@ -276,6 +345,17 @@
         device_id_type=MESH,
     ).wait_recv()
 
+    @pl.when(crossing)
+    def _():
+        pltpu.make_async_remote_copy(
+            src_ref=row_ref.at[1],
+            dst_ref=col_ref.at[1],
+            send_sem=sends.at[1],
+            recv_sem=recvb.at[1],
+            device_id=(f, 1 - r, 2 * k + 1),
+            device_id_type=MESH,
+        ).wait_recv()
+
     @pl.when(jnp.logical_not(crossing))
     def _():
         half = pltpu.make_async_copy(row_ref.at[pl.ds(2 * k, 2)], col_ref, local_sem)
@@ -289,16 +369,19 @@
     lax.fori_loop(1, nf, wait_send_freq, 0)
     to_sib.wait_send()
     to_cross.wait_send()
+    fan_copy(base + mine).wait_send()
+
+    @pl.when(side_source)
+    def _():
+        side_copy().wait_send()
 
     @pl.when(crossing)
     def _():
-        for e in range(2):
-            relay_copy(e).wait_send()
-
-    @pl.when(relay_target)
-    def _():
-        for e in range(2):
-            fan_copy(e, 2 * (2 - c)).wait_send()
+        relay_copy().wait_send()
+
+    @pl.when(side_relay)
+    def _():
+        side_relay_copy().wait_send()
 
 
 def fused_call(samples, gains, taps, table):
@@ -327,6 +410,7 @@
             pltpu.VMEM((2 * NFFT // LANES, SPEC * inputs_here, LANES), jnp.float32),
             pltpu.VMEM((channels * inputs_here, width), jnp.float32),
             pltpu.VMEM((nf, rows, width), jnp.bfloat16),
+            pltpu.VMEM((nf, rows, width), jnp.bfloat16),
             pltpu.SemaphoreType.DMA((7,)),
             pltpu.SemaphoreType.DMA((nf,)),
             pltpu.SemaphoreType.DMA((nf,)),
@@ -334,8 +418,10 @@
             pltpu.SemaphoreType.DMA((6,)),
             pltpu.SemaphoreType.DMA,
             pltpu.SemaphoreType.DMA((2,)),
-            pltpu.SemaphoreType.DMA((2,)),
-            pltpu.SemaphoreType.DMA((2,)),
+            pltpu.SemaphoreType.DMA,
+            pltpu.SemaphoreType.DMA,
+            pltpu.SemaphoreType.DMA,
+            pltpu.SemaphoreType.DMA,
             pltpu.SemaphoreType.DMA,
         ],
         compiler_params=pltpu.CompilerParams(

time: 48.5 us -> 46 us (0.948)
  Pallas kernels: 47.7 us -> 45.2 us
    pallas_call x1, Pallas kernels: 41.6 us -> 39.1 us  [fused_call(): pl.pallas_call(fused_kernel, out_shape=(jax.ShapeDtypeStruct((ncol, nf, r...]
where the time goes in v11:
time: 46 us; the launch traced here: 45.9 us
  Pallas kernels  45.2 us (98%)
  between operations  0.64 us (1%)
    pallas_call x1, Pallas kernels, fused_call(): pl.pallas_call(fused_kernel, out_shape=(jax.ShapeDtypeStruct((ncol, nf, r...  39.1 us
    pallas_call x1, Pallas kernels, visibilities(): pl.pallas_call(vis_kernel, grid=(CH_DEV,), out_shape=(out, out), in_specs...  6.1 us

profile of v11, /device:TPU:1, one launch (start us, length us, event | category | flops | bytes accessed | tf_op | source)
XLA Modules:
  0.0 45.9 jit_solution(13479479495882451501)
XLA Ops:
  0.6 39.1 %shard_map.59 = (bf16[4,32,32,128]{3,2,1,0:T(8,128)(2,1)}, bf16[2,32,32,128]{3,2,1,0:T(8,128)(2,1)}) custom-call(f32[8]{0:T(128)} %g_hbm.1, f32[4,1024]{1,0:T(4,128)} %taps_hbm.1, s32[2,8,68608]{2,1,0:T(8,128)} %s_hbm.1, bf16[256,2048]{1,0:T(8,128)(2,1)} %constant.2.clone.tab_hbm), custom_call_target="tpu_custom_call" | custom-call | tf_op jit(solution)/shard_map/pallas_call | solution.py:396
  39.8 6.1 %shard_map.60 = (bf16[4,1024,512]{2,1,0:T(8,128)(2,1)}, bf16[4,1024,512]{2,1,0:T(8,128)(2,1)}) custom-call(bf16[4,32,32,128]{3,2,1,0:T(8,128)(2,1)} %get-tuple-element.4.row_ref, bf16[2,32,32,128]{3,2,1,0:T(8,128)(2,1)} %get-tuple-element.5.col_ref), custom_call_target="tpu_custom_call" | custom-call | tf_op jit(solution)/shard_map/pallas_call | solution.py:471

commit v12 on v11

--- a/solution.py
+++ b/solution.py
@@ -442,24 +442,25 @@
 def vis_kernel(row_ref, col_ref, vr_ref, vi_ref, a_scr, b_scr):
     kk = pl.program_id(0)
     groups = row_ref.shape[2] // CH_DEV
-
-    @pl.when(kk == 0)
-    def _():
-        rows = row_ref[...].astype(jnp.float32)
-        cols = col_ref[...].astype(jnp.float32)
-        for j in range(CH_DEV):
+    pair = pl.multiple_of((kk // 2) * 2 * groups, 2 * groups)
+    rows = row_ref[:, :, pl.ds(pair, 2 * groups), :].astype(jnp.float32)
+    cols = col_ref[:, :, pl.ds(pair, 2 * groups), :].astype(jnp.float32)
+    for j in range(2):
+
+        @pl.when(kk % 2 == j)
+        def _():
             a = rows[:, :, j * groups : (j + 1) * groups, :]
-            a_scr[j] = a.reshape(-1, a.shape[-1]).astype(a_scr.dtype)
+            a_scr[...] = a.reshape(-1, a.shape[-1]).astype(a_scr.dtype)
             b = cols[:, :, j * groups : (j + 1) * groups, :]
             b = b.reshape(-1, b.shape[-1])
-            b_scr[j, 0] = b.astype(b_scr.dtype)
-            b_scr[j, 1] = jnp.concatenate([-b[:, SPEC:], b[:, :SPEC]], axis=1).astype(b_scr.dtype)
-
-    a = a_scr[kk]
+            b_scr[0] = b.astype(b_scr.dtype)
+            b_scr[1] = jnp.concatenate([-b[:, SPEC:], b[:, :SPEC]], axis=1).astype(b_scr.dtype)
+
+    a = a_scr[...]
     dims = (((1,), (1,)), ((), ()))
-    vr = lax.dot_general(a, b_scr[kk, 0], dims, preferred_element_type=jnp.float32)
+    vr = lax.dot_general(a, b_scr[0], dims, preferred_element_type=jnp.float32)
     vr_ref[0] = (vr * (1.0 / SPEC)).astype(vr_ref.dtype)
-    vi = lax.dot_general(a, b_scr[kk, 1], dims, preferred_element_type=jnp.float32)
+    vi = lax.dot_general(a, b_scr[1], dims, preferred_element_type=jnp.float32)
     vi_ref[0] = (vi * (1.0 / SPEC)).astype(vi_ref.dtype)
 
 
@@ -481,8 +482,8 @@
             pl.BlockSpec((1, nrow, ncolumn), lambda k: (k, 0, 0)),
         ),
         scratch_shapes=[
-            pltpu.VMEM((CH_DEV, nrow, width), jnp.bfloat16),
-            pltpu.VMEM((CH_DEV, 2, ncolumn, width), jnp.bfloat16),
+            pltpu.VMEM((nrow, width), jnp.bfloat16),
+            pltpu.VMEM((2, ncolumn, width), jnp.bfloat16),
         ],
         compiler_params=pltpu.CompilerParams(vmem_limit_bytes=63 * 1024 * 1024),
     )(row_blk, col_blk)

time: 46 us -> 46.3 us (level)
  no operation moved by 1% of the time
where the time goes in v12:
time: 46.3 us; the launch traced here: 46.1 us
  Pallas kernels  45.5 us (98%)
  between operations  0.64 us (1%)
    pallas_call x1, Pallas kernels, fused_call(): pl.pallas_call(fused_kernel, out_shape=(jax.ShapeDtypeStruct((ncol, nf, r...  39.1 us
    pallas_call x1, Pallas kernels, visibilities(): pl.pallas_call(vis_kernel, grid=(CH_DEV,), out_shape=(out, out), in_specs...  6.36 us

profile of v12, /device:TPU:1, one launch (start us, length us, event | category | flops | bytes accessed | tf_op | source)
XLA Modules:
  0.0 46.1 jit_solution(13258394931375628532)
XLA Ops:
  0.6 39.1 %shard_map.59 = (bf16[4,32,32,128]{3,2,1,0:T(8,128)(2,1)}, bf16[2,32,32,128]{3,2,1,0:T(8,128)(2,1)}) custom-call(f32[8]{0:T(128)} %g_hbm.1, f32[4,1024]{1,0:T(4,128)} %taps_hbm.1, s32[2,8,68608]{2,1,0:T(8,128)} %s_hbm.1, bf16[256,2048]{1,0:T(8,128)(2,1)} %constant.2.clone.tab_hbm), custom_call_target="tpu_custom_call" | custom-call | tf_op jit(solution)/shard_map/pallas_call | solution.py:396
  39.8 6.4 %shard_map.60 = (bf16[4,1024,512]{2,1,0:T(8,128)(2,1)}, bf16[4,1024,512]{2,1,0:T(8,128)(2,1)}) custom-call(bf16[4,32,32,128]{3,2,1,0:T(8,128)(2,1)} %get-tuple-element.4.row_ref, bf16[2,32,32,128]{3,2,1,0:T(8,128)(2,1)} %get-tuple-element.5.col_ref), custom_call_target="tpu_custom_call" | custom-call | tf_op jit(solution)/shard_map/pallas_call | solution.py:472

commit v13 on v12

--- a/solution.py
+++ b/solution.py
@@ -450,7 +450,7 @@
         @pl.when(kk % 2 == j)
         def _():
             a = rows[:, :, j * groups : (j + 1) * groups, :]
-            a_scr[...] = a.reshape(-1, a.shape[-1]).astype(a_scr.dtype)
+            a_scr[...] = (a.reshape(-1, a.shape[-1]) * (1.0 / SPEC)).astype(a_scr.dtype)
             b = cols[:, :, j * groups : (j + 1) * groups, :]
             b = b.reshape(-1, b.shape[-1])
             b_scr[0] = b.astype(b_scr.dtype)
@@ -459,9 +459,9 @@
     a = a_scr[...]
     dims = (((1,), (1,)), ((), ()))
     vr = lax.dot_general(a, b_scr[0], dims, preferred_element_type=jnp.float32)
-    vr_ref[0] = (vr * (1.0 / SPEC)).astype(vr_ref.dtype)
+    vr_ref[0] = vr.astype(vr_ref.dtype)
     vi = lax.dot_general(a, b_scr[1], dims, preferred_element_type=jnp.float32)
-    vi_ref[0] = (vi * (1.0 / SPEC)).astype(vi_ref.dtype)
+    vi_ref[0] = vi.astype(vi_ref.dtype)
 
 
 def visibilities(row_blk, col_blk):

time: 46.3 us -> 46.2 us (level)
  no operation moved by 1% of the time
where the time goes in v13:
time: 46.2 us; the launch traced here: 46.1 us
  Pallas kernels  45.4 us (98%)
  between operations  0.64 us (1%)
    pallas_call x1, Pallas kernels, fused_call(): pl.pallas_call(fused_kernel, out_shape=(jax.ShapeDtypeStruct((ncol, nf, r...  39.1 us
    pallas_call x1, Pallas kernels, visibilities(): pl.pallas_call(vis_kernel, grid=(CH_DEV,), out_shape=(out, out), in_specs...  6.31 us

profile of v13, /device:TPU:1, one launch (start us, length us, event | category | flops | bytes accessed | tf_op | source)
XLA Modules:
  0.0 46.1 jit_solution(15474018669846497828)
XLA Ops:
  0.6 39.1 %shard_map.59 = (bf16[4,32,32,128]{3,2,1,0:T(8,128)(2,1)}, bf16[2,32,32,128]{3,2,1,0:T(8,128)(2,1)}) custom-call(f32[8]{0:T(128)} %g_hbm.1, f32[4,1024]{1,0:T(4,128)} %taps_hbm.1, s32[2,8,68608]{2,1,0:T(8,128)} %s_hbm.1, bf16[256,2048]{1,0:T(8,128)(2,1)} %constant.2.clone.tab_hbm), custom_call_target="tpu_custom_call" | custom-call | tf_op jit(solution)/shard_map/pallas_call | solution.py:396
  39.8 6.3 %shard_map.60 = (bf16[4,1024,512]{2,1,0:T(8,128)(2,1)}, bf16[4,1024,512]{2,1,0:T(8,128)(2,1)}) custom-call(bf16[4,32,32,128]{3,2,1,0:T(8,128)(2,1)} %get-tuple-element.4.row_ref, bf16[2,32,32,128]{3,2,1,0:T(8,128)(2,1)} %get-tuple-element.5.col_ref), custom_call_target="tpu_custom_call" | custom-call | tf_op jit(solution)/shard_map/pallas_call | solution.py:472

commit v14 on v13

--- a/solution.py
+++ b/solution.py
@@ -75,11 +75,13 @@
 
         lax.fori_loop(lo, hi, body, 0)
 
+    coef = [jnp.broadcast_to(taps_ref[t : t + 1, :], (inputs_here, NFFT)) for t in range(TAPS)]
+
     def filt(p, lo, hi):
         def body(m, carry):
-            total = vbuf[p, m] * taps_ref[0:1, :]
+            total = vbuf[p, m] * coef[0]
             for t in range(1, TAPS):
-                total = total + vbuf[p, m + t] * taps_ref[t : t + 1, :]
+                total = total + vbuf[p, m + t] * coef[t]
             rows = pl.ds(pl.multiple_of(m * inputs_here, inputs_here), inputs_here)
             for b in range(blocks):
                 f_ref[p * blocks + b, rows, :] = total[:, b * LANES : (b + 1) * LANES]

time: 46.2 us -> 45.8 us (level)
  no operation moved by 1% of the time
where the time goes in v14:
time: 45.8 us; the launch traced here: 45.7 us
  Pallas kernels  45 us (98%)
  between operations  0.64 us (1%)
    pallas_call x1, Pallas kernels, fused_call(): pl.pallas_call(fused_kernel, out_shape=(jax.ShapeDtypeStruct((ncol, nf, r...  38.7 us
    pallas_call x1, Pallas kernels, visibilities(): pl.pallas_call(vis_kernel, grid=(CH_DEV,), out_shape=(out, out), in_specs...  6.31 us

profile of v14, /device:TPU:1, one launch (start us, length us, event | category | flops | bytes accessed | tf_op | source)
XLA Modules:
  0.0 45.7 jit_solution(12759945630445682984)
XLA Ops:
  0.6 38.7 %shard_map.59 = (bf16[4,32,32,128]{3,2,1,0:T(8,128)(2,1)}, bf16[2,32,32,128]{3,2,1,0:T(8,128)(2,1)}) custom-call(f32[8]{0:T(128)} %g_hbm.1, f32[4,1024]{1,0:T(4,128)} %taps_hbm.1, s32[2,8,68608]{2,1,0:T(8,128)} %s_hbm.1, bf16[256,2048]{1,0:T(8,128)(2,1)} %constant.2.clone.tab_hbm), custom_call_target="tpu_custom_call" | custom-call | tf_op jit(solution)/shard_map/pallas_call | solution.py:398
  39.4 6.3 %shard_map.60 = (bf16[4,1024,512]{2,1,0:T(8,128)(2,1)}, bf16[4,1024,512]{2,1,0:T(8,128)(2,1)}) custom-call(bf16[4,32,32,128]{3,2,1,0:T(8,128)(2,1)} %get-tuple-element.4.row_ref, bf16[2,32,32,128]{3,2,1,0:T(8,128)(2,1)} %get-tuple-element.5.col_ref), custom_call_target="tpu_custom_call" | custom-call | tf_op jit(solution)/shard_map/pallas_call | solution.py:474
